TPU v7x, 32 devices: a whole 2x2x4 slice. The times are simulated.
32 devices in a mesh: ctx: 8 (over y, x, core), tp: 4 (over z).
Axes of the slice: x: 2, y: 2, z: 4, core: 2. Of those that a mesh axis runs over, the one named last changes fastest.
Arguments:
- queries: bfloat16 [2048, 4096], P('ctx', 'tp'), may hold values from -6 to 6
- attn_keys: bfloat16 [2048, 4096], P('ctx', 'tp'), may hold values from -6 to 6
- attn_values: bfloat16 [2048, 4096], P('ctx', 'tp'), may hold values from -6 to 6
- out_proj: bfloat16 [4096, 8192], P('tp'), may hold values from -0.25 to 0.25
Outputs:
- mixed: bfloat16 [2048, 8192], P('ctx', 'tp')
All inputs are finite; a program needn't handle non-finite values.
Results may differ from a plain program's by a relative error of at most 0.013.
Values may be sent and summed in bfloat16 or wider, within the bound.
No kernel may reach another device: no remote copies, remote signals or barrier semaphores. Data moves between devices by JAX's collectives and lax.ppermute only.
A program may use at most 256 MiB of HBM per device.

v0:
```python
import jax
import jax.numpy as jnp
from jax import lax
from jax.sharding import PartitionSpec as P

HS = 128


def attend(carry, query_set, query_pos, key_piece, value_piece, key_pos):
    run_max, run_sum, run_acc = carry
    pieces = key_piece.shape[0]
    heads_local = query_set.shape[1]
    key_heads = key_piece.reshape(pieces, heads_local, HS)
    value_heads = value_piece.reshape(pieces, heads_local, HS)
    scores = jnp.einsum("rhd,phd->hrp", query_set, key_heads, preferred_element_type=jnp.float32)
    scores = scores * (1.0 / HS**0.5)
    visible = key_pos[None, None, :] <= query_pos[None, :, None]
    scores = jnp.where(visible, scores, -1e30)
    new_max = jnp.maximum(run_max, jnp.max(scores, axis=2))
    weights = jnp.where(visible, jnp.exp(scores - new_max[:, :, None]), 0.0)
    new_sum = jnp.sum(weights, axis=2)
    update = jnp.einsum(
        "hrp,phd->rhd",
        weights.astype(jnp.bfloat16),
        value_heads,
        preferred_element_type=jnp.float32,
    )
    return (new_max, new_sum, update)


def start_carry(heads_local, rows_count):
    return (
        jnp.full((heads_local, rows_count), -1e30, jnp.float32),
        jnp.zeros((heads_local, rows_count), jnp.float32),
        jnp.zeros((rows_count, heads_local, HS), jnp.float32),
    )


def body(queries, attn_keys, attn_values, out_proj):
    ctx_count = lax.axis_size("ctx")
    ctx_index = lax.axis_index("ctx")
    tok_dev = queries.shape[0]
    half_len = tok_dev // 2
    heads_local = queries.shape[1] // HS
    query_heads = queries.reshape(tok_dev, heads_local, HS)
    offsets = jnp.arange(half_len, dtype=jnp.int32)
    query_pos = jnp.concatenate(
        [ctx_index * half_len + offsets, (2 * ctx_count - 1 - ctx_index) * half_len + offsets]
    )
    key_piece = lax.all_gather(attn_keys, "ctx", axis=0, tiled=True)
    value_piece = lax.all_gather(attn_values, "ctx", axis=0, tiled=True)
    stored = jnp.arange(key_piece.shape[0], dtype=jnp.int32)
    device = stored // tok_dev
    within = stored % tok_dev
    key_pos = jnp.where(
        within < half_len,
        device * half_len + within,
        (2 * ctx_count - 1 - device) * half_len + within - half_len,
    )
    run_max, run_sum, run_acc = attend(
        start_carry(heads_local, tok_dev), query_heads, query_pos, key_piece, value_piece, key_pos
    )
    attended = (run_acc / jnp.transpose(run_sum)[:, :, None]).reshape(tok_dev, heads_local * HS)
    attended = attended.astype(jnp.bfloat16)
    partial_value = jnp.dot(attended, out_proj, preferred_element_type=jnp.float32).astype(
        jnp.bfloat16
    )
    share = lax.psum_scatter(
        partial_value.astype(jnp.float32).astype(jnp.bfloat16),
        "tp",
        scatter_dimension=1,
        tiled=True,
    )
    return share


def solution(mesh):
    in_specs = (P("ctx", "tp"), P("ctx", "tp"), P("ctx", "tp"), P("tp", None))
    out_specs = P("ctx", "tp")
    return jax.shard_map(body, mesh=mesh, in_specs=in_specs, out_specs=out_specs, check_vma=False)
```

profile of v0, /device:TPU:0, one launch (start us, length us, event | category | flops | bytes accessed | tf_op | source)
XLA Modules:
  0.0 199.7 jit_solution(17762131553983659850)
XLA Ops:
  6.5 0.0 copy-start
  6.5 0.0 all-gather.3.cloned.1.call-start
  6.5 2.1 %copy.7 = bf16[256,1024]{0,1:T(8,128)(2,1)} copy(bf16[256,1024]{1,0:T(8,128)(2,1)} %param.5) | data formatting | bytes 1048576 | tf_op args[1]
  8.6 0.0 all-gather.3.cloned.1.call-update
  8.7 0.0 all-gather.5.cloned.1.call-start
  8.7 0.7 all-gather.5.cloned.1.call-update
  9.4 0.0 reduce-scatter.2.cloned.1.call-start
  9.5 0.4 broadcast_compare_fusion
  9.9 39.4 %all-gather.3.cloned.1.call-done = bf16[2048,1024]{0,1:T(8,128)(2,1)} async-done(((bf16[256,1024]{0,1:T(8,128)(2,1)}), bf16[2048,1024]{0,1:T(8,128)(2,1)}) %all-gather.3.cloned.1.call-update) | async-done | bytes 4194320 | tf_op jit(solution)/shard_map/all_gather | solution.py:50
  49.3 0.0 copy-done
  49.3 5.3 %fusion = (f32[8,256]{1,0:T(8,128)S(1)}, f32[8,256,2048]{2,1,0:T(8,128)S(1)}) fusion(pred[256,2048]{1,0:T(8,128)(4,1)S(1)} %broadcast_compare_fusion, bf16[2048,8,128]{0,2,1:T(8,128)(2,1)} %bitcast.21, bf16[256,1024]{1,0:T(8,128)(2,1)S(1)} %copy-done), kind=kOutput, calls=%fused_computation.2 | convolution fusion | flops 1086322688 | bytes 22028288 | tf_op jit(solution)/shard_map/rhd,phd->hrp/dot_general | solution.py:15
  54.6 0.0 copy-start.1
  54.6 6.1 %copy-done.1 = f32[8,256,2048]{2,1,0:T(8,128)} copy-done((f32[8,256,2048]{2,1,0:T(8,128)}, f32[8,256,2048]{2,1,0:T(8,128)S(1)}, u32[]{:S(2)}) %copy-start.1) | copy-done | bytes 16777240
  60.7 5.0 %fusion.1 = f32[8,256]{1,0:T(8,128)S(1)} fusion(f32[8,256,2048]{2,1,0:T(8,128)S(1)} %get-tuple-element.6, f32[8,256]{1,0:T(8,128)S(1)} %broadcast_maximum_fusion, pred[256,2048]{1,0:T(8,128)(4,1)S(1)} %broadcast_compare_fusion), kind=kLoop, calls=%fused_computation.3 | loop fusion | flops 20969472 | bytes 17317888 | tf_op jit(solution)/shard_map/reduce_sum | solution.py:21
  65.7 22.1 %all-gather.5.cloned.1.call-done = bf16[2048,1024]{1,0:T(8,128)(2,1)} async-done(((bf16[256,1024]{1,0:T(8,128)(2,1)}), bf16[2048,1024]{1,0:T(8,128)(2,1)}) %all-gather.5.cloned.1.call-update) | async-done | bytes 4194320 | tf_op jit(solution)/shard_map/all_gather | solution.py:51
  87.8 6.5 %copy.10 = bf16[2048,1024]{0,1:T(8,128)(2,1)} copy(bf16[2048,1024]{1,0:T(8,128)(2,1)} %all-gather.5.cloned.1.call-done) | data formatting | bytes 8388608 | tf_op jit(solution)/shard_map/all_gather | solution.py:51
  94.3 9.8 %divide_convert_fusion = bf16[256,8,128]{0,2,1:T(8,128)(2,1)S(1)} fusion(bf16[2048,8,128]{0,2,1:T(8,128)(2,1)} %bitcast.22, f32[8,256,2048]{2,1,0:T(8,128)} %copy-done.1, f32[8,256]{1,0:T(8,128)S(1)} %broadcast_maximum_fusion, pred[256,2048]{1,0:T(8,128)(4,1)S(1)} %broadcast_compare_fusion, f32[256,8]{0,1:T(8,128)S(1)} %bitcast.24), kind=kOutput, calls=%fused_computation.9 | convolution fusion | flops 1095237632 | bytes 22036480 | tf_op jit(solution)/shard_map/hrp,phd->rhd/dot_general | solution.py:22
  104.2 12.1 %convolution_convert_fusion = bf16[256,8192]{1,0:T(8,128)(2,1)} fusion(bf16[256,1024]{0,1:T(8,128)(2,1)S(1)} %bitcast.23, bf16[1024,8192]{1,0:T(8,128)(2,1)} %param.7), kind=kOutput, calls=%fused_computation.5 | convolution fusion | flops 4297064448 | bytes 21495808 | tf_op jit(solution)/shard_map/dot_general | solution.py:65
  116.2 0.0 reduce-scatter.2.cloned.1.call-update
  116.3 76.9 %reduce-scatter.2.cloned.1.call-done = bf16[256,2048]{1,0:T(8,128)(2,1)} async-done(((bf16[256,8192]{1,0:T(8,128)(2,1)}), bf16[256,2048]{1,0:T(8,128)(2,1)}) %reduce-scatter.2.cloned.1.call-update) | async-done | bytes 1048592 | tf_op jit(solution)/shard_map/reduce_scatter | solution.py:68
  (4 shorter events, 0.0 us)
Async XLA Ops:
  6.5 42.8 %copy-start = (bf16[256,1024]{1,0:T(8,128)(2,1)S(1)}, bf16[256,1024]{1,0:T(8,128)(2,1)}, u32[]{:S(2)}) copy-start(bf16[256,1024]{1,0:T(8,128)(2,1)} %param.4) | copy-start | bytes 1572868
  6.5 42.8 %all-gather.3.cloned.1.call-start = ((), (), s32[]{:S(2)}) async-start(), calls=%async_computation.1 | async-start | bytes 4718592 | tf_op jit(solution)/shard_map/all_gather | solution.py:50
  8.7 79.1 %all-gather.5.cloned.1.call-start = ((), (), s32[]{:S(2)}) async-start(), calls=%async_computation.2 | async-start | bytes 4718592 | tf_op jit(solution)/shard_map/all_gather | solution.py:51
  9.4 183.8 %reduce-scatter.2.cloned.1.call-start = ((), (), s32[]{:S(2)}) async-start(), calls=%async_computation.3 | async-start | bytes 5242880 | tf_op jit(solution)/shard_map/reduce_scatter | solution.py:68
  54.6 6.1 %copy-start.1 = (f32[8,256,2048]{2,1,0:T(8,128)}, f32[8,256,2048]{2,1,0:T(8,128)S(1)}, u32[]{:S(2)}) copy-start(f32[8,256,2048]{2,1,0:T(8,128)S(1)} %get-tuple-element.6) | copy-start | bytes 50331652
Sparse Core Ops, SparseCore 0:
  9.2 40.0 all-gather.2
  51.2 36.5 all-gather.4
  116.4 76.7 reduce-scatter.1
where the time goes:
time: 200 us
  waiting for transfers between devices  139 us (70%)
  matrix products  27.2 us (14%)
  local copies, waits for them, and re-layouts  14.7 us (7%)
  between operations  13.2 us (7%)
  other arithmetic  5.4 us (3%)
    reduce_scatter x1, waiting for transfers between devices, body(): lax.psum_scatter(partial_value.astype(jnp.float32).astype(jnp.bfloat16),...  76.9 us
    all_gather x1, waiting for transfers between devices, body(): key_piece = lax.all_gather(attn_keys, 'ctx', axis=0, tiled=True)  39.4 us
    all_gather x1, waiting for transfers between devices, body(): value_piece = lax.all_gather(attn_values, 'ctx', axis=0, tiled=True)  22.1 us
    dot_general x1, matrix products, body(): jnp.dot(attended, out_proj, preferred_element_type=jnp.float32)  12.1 us
    dot_general x1, matrix products, attend(): jnp.einsum('hrp,phd->rhd', weights.astype(jnp.bfloat16), value_heads, pre...  9.81 us
    unnamed x5, local copies, waits for them, and re-layouts  8.17 us
    all_gather x1, local copies, waits for them, and re-layouts, body(): value_piece = lax.all_gather(attn_values, 'ctx', axis=0, tiled=True)  6.52 us
    dot_general x1, matrix products, attend(): jnp.einsum('rhd,phd->hrp', query_set, key_heads, preferred_element_type=j...  5.27 us
  transfers between devices with their start and end apart: 3, of which 3 were waited for; matrix products, arithmetic and copies ran while one was open for 5% of the time, Pallas kernels for 0%

commit v1 on v0

v1 whole, which is shorter than its diff:
```python
import functools
import math

import jax
import jax.numpy as jnp
from jax import lax
from jax.experimental import pallas as pl
from jax.experimental.pallas import tpu as pltpu
from jax.sharding import PartitionSpec as P


HS = 128
ANY = pl.BlockSpec(memory_space=pl.ANY)
HBM = pl.BlockSpec(memory_space=pltpu.HBM)
VMEM = pl.BlockSpec(memory_space=pltpu.VMEM)
COPIES = pltpu.CompilerParams(vmem_limit_bytes=1 << 20)
PARAMS = pltpu.CompilerParams(vmem_limit_bytes=8 << 20)


def gathered_attention(queries, attn_keys, attn_values):
    ctx_count = lax.axis_size("ctx")
    ctx_index = lax.axis_index("ctx")
    tok_dev = queries.shape[0]
    half_len = tok_dev // 2
    heads_local = queries.shape[1] // HS
    query_heads = queries.reshape(tok_dev, heads_local, HS)
    offsets = jnp.arange(half_len, dtype=jnp.int32)
    query_pos = jnp.concatenate(
        [ctx_index * half_len + offsets, (2 * ctx_count - 1 - ctx_index) * half_len + offsets]
    )
    key_heads = lax.all_gather(attn_keys, "ctx", axis=0, tiled=True).reshape(-1, heads_local, HS)
    value_heads = lax.all_gather(attn_values, "ctx", axis=0, tiled=True).reshape(-1, heads_local, HS)
    stored = jnp.arange(key_heads.shape[0], dtype=jnp.int32)
    device = stored // tok_dev
    within = stored % tok_dev
    key_pos = jnp.where(
        within < half_len,
        device * half_len + within,
        (2 * ctx_count - 1 - device) * half_len + within - half_len,
    )
    scores = jnp.einsum("rhd,phd->hrp", query_heads, key_heads, preferred_element_type=jnp.float32)
    scores = scores * (1.0 / HS**0.5)
    visible = key_pos[None, None, :] <= query_pos[None, :, None]
    scores = jnp.where(visible, scores, -1e30)
    top = jnp.max(scores, axis=2, keepdims=True)
    weights = jnp.where(visible, jnp.exp(scores - top), 0.0)
    total = jnp.sum(weights, axis=2)
    update = jnp.einsum(
        "hrp,phd->rhd", weights.astype(jnp.bfloat16), value_heads, preferred_element_type=jnp.float32
    )
    attended = update / jnp.transpose(total)[:, :, None]
    return attended.reshape(tok_dev, heads_local * HS).astype(jnp.bfloat16)


def general_body(queries, attn_keys, attn_values, out_proj):
    attended = gathered_attention(queries, attn_keys, attn_values)
    partial_value = jnp.dot(attended, out_proj, preferred_element_type=jnp.float32).astype(
        jnp.bfloat16
    )
    return lax.psum_scatter(partial_value, "tp", scatter_dimension=1, tiled=True)


def my_group():
    return lax.axis_index("ctx") // 2


def run_copies(pairs, sems):
    copies = [pltpu.make_async_copy(src, dst, sems.at[i]) for i, (src, dst) in enumerate(pairs)]
    for copy in copies:
        copy.start()
    for copy in copies:
        copy.wait()


def pack_kernel(row0, q_ref, k_ref, v_ref, *rest):
    outs, sems = rest[:-1], rest[-1]
    half, width = outs[0].shape[1:]
    pairs = []
    for j, out in enumerate(outs):
        column = pl.multiple_of(lax.bitwise_xor(my_group(), j) * width, width)
        for i, ref in enumerate((q_ref, k_ref, v_ref)):
            pairs.append((ref.at[pl.ds(row0, half), pl.ds(column, width)], out.at[i]))
    run_copies(pairs, sems)


def pack(queries, attn_keys, attn_values, row0, half, groups):
    width = queries.shape[1] // groups
    out = jax.ShapeDtypeStruct((3, half, width), queries.dtype)
    return pl.pallas_call(
        functools.partial(pack_kernel, row0),
        out_shape=[out] * groups,
        in_specs=[HBM] * 3,
        out_specs=[VMEM] * groups,
        scratch_shapes=[pltpu.SemaphoreType.DMA((3 * groups,))],
        compiler_params=COPIES,
        cost_estimate=pl.CostEstimate(
            flops=0, bytes_accessed=6 * half * width * groups * 2, transcendentals=0
        ),
    )(queries, attn_keys, attn_values)


def piece_kernel(tp_count, w_ref, out_ref, sems):
    width = out_ref.shape[1]
    z = lax.axis_index("tp")
    target = jnp.where(z == 0, 1, tp_count - 2)
    column = target * (w_ref.shape[1] // tp_count) + lax.axis_index("ctx") * width
    column = pl.multiple_of(column, width)
    run_copies([(w_ref.at[:, pl.ds(column, width)], out_ref)], sems)


def piece(out_proj, tp_count, ctx_count):
    width = out_proj.shape[1] // tp_count // ctx_count
    return pl.pallas_call(
        functools.partial(piece_kernel, tp_count),
        out_shape=jax.ShapeDtypeStruct((out_proj.shape[0], width), out_proj.dtype),
        in_specs=[HBM],
        out_specs=VMEM,
        scratch_shapes=[pltpu.SemaphoreType.DMA((1,))],
        name="piece",
        compiler_params=COPIES,
        cost_estimate=pl.CostEstimate(
            flops=0, bytes_accessed=4 * out_proj.shape[0] * width, transcendentals=0
        ),
    )(out_proj)


def attend(groups, phases, group, core, ins, outs):
    half, width = outs[0].shape
    rate = math.log2(math.e) / HS**0.5
    per_phase = groups + 1
    row = lax.broadcasted_iota(jnp.int32, (half, 2 * half), 0)
    col = lax.broadcasted_iota(jnp.int32, (half, 2 * half), 1)
    other_seen = core == (1 if phases == 1 else 0)
    visible = col < jnp.where(other_seen, 2 * half, half)
    visible = visible & ((col >= half) | (col <= row))
    contract = (((1,), (1,)), ((), ()))
    every = list(range(groups))

    tiles = []
    for phase in range(phases):
        for at in every:
            if phase < phases - 1:
                tiles.append((phase, at, every))
            elif phases == 1:
                tiles.append((phase, at, every[at:]))
            else:
                tiles.append((phase, at, every[: at + 1]))

    def keys_of(phase, at, which, lanes):
        own = ins[phase * per_phase + (at ^ group)]
        other = ins[phase * per_phase + groups]
        return jnp.concatenate(
            [own[which, :, lanes], other[at ^ group, which - 1, :, lanes]], axis=0
        )

    def rows(array, i):
        return array[i * half : (i + 1) * half]

    for head in range(width // HS):
        lanes = slice(head * HS, (head + 1) * HS)
        query = {
            at: ins[(phases - 1) * per_phase + (at ^ group)][0, :, lanes] for at in every
        }
        scores, best, total, acc = {}, {}, {}, {}
        for phase, at, seen in tiles:
            tall = jnp.concatenate([query[a] for a in seen], axis=0)
            dot = lax.dot_general(
                tall, keys_of(phase, at, 1, lanes), contract, preferred_element_type=jnp.float32
            )
            for i, a in enumerate(seen):
                mine = rows(dot, i)
                if a == at and phase == phases - 1:
                    mine = jnp.where(visible, mine, -1e30)
                scores[phase, at, a] = mine
                best[a] = jnp.maximum(best[a], mine) if a in best else mine
        top = {a: jnp.max(best[a], axis=1, keepdims=True) for a in every}
        for phase, at, seen in tiles:
            weights = []
            for a in seen:
                mine = jnp.exp2((scores[phase, at, a] - top[a]) * rate)
                total[a] = total[a] + mine if a in total else mine
                weights.append(mine.astype(jnp.bfloat16))
            dot = jnp.dot(
                jnp.concatenate(weights, axis=0),
                keys_of(phase, at, 2, lanes),
                preferred_element_type=jnp.float32,
            )
            for i, a in enumerate(seen):
                mine = rows(dot, i)
                acc[a] = acc[a] + mine if a in acc else mine
        for a in every:
            out = acc[a] / jnp.sum(total[a], axis=1, keepdims=True)
            outs[a ^ group][:, lanes] = out.astype(outs[0].dtype)


def attention_kernel(groups, phases, *refs):
    ins, outs = refs[:-groups], refs[-groups:]
    core = lax.rem(lax.axis_index("ctx"), 2)
    for group in range(groups):

        @pl.when(my_group() == group)
        def _(group=group):
            attend(groups, phases, group, core, ins, outs)


def attention(phase_inputs, groups, half, width):
    phases = len(phase_inputs)
    flat = [array for own, other in phase_inputs for array in (*own, other)]
    out = jax.ShapeDtypeStruct((half, width), jnp.bfloat16)
    elements = groups * width // HS * half * half * (groups + 1 if phases == 1 else 3 * groups + 1)
    return pl.pallas_call(
        functools.partial(attention_kernel, groups, phases),
        out_shape=[out] * groups,
        in_specs=[VMEM] * len(flat),
        out_specs=[VMEM] * groups,
        compiler_params=PARAMS,
        cost_estimate=pl.CostEstimate(
            flops=4 * HS * elements, bytes_accessed=2 << 20, transcendentals=elements
        ),
    )(*flat)


def hold_kernel(place_ref, w_ref, out_ref, sems):
    columns, count = out_ref.shape[1], sems.shape[0]
    rows = out_ref.shape[0] // count
    at = pl.ds(pl.multiple_of(place_ref[0] * columns, columns), columns)
    pairs = []
    for i in range(count):
        band = pl.ds(i * rows, rows)
        pairs.append((w_ref.at[band, at], out_ref.at[band, :]))
    run_copies(pairs, sems)


def hold(out_proj, target, tp_count):
    rows, columns = out_proj.shape[0], out_proj.shape[1] // tp_count
    return pl.pallas_call(
        hold_kernel,
        out_shape=jax.ShapeDtypeStruct((rows, columns), out_proj.dtype),
        grid_spec=pltpu.PrefetchScalarGridSpec(
            num_scalar_prefetch=1,
            grid=(),
            in_specs=[HBM],
            out_specs=VMEM,
            scratch_shapes=[pltpu.SemaphoreType.DMA((16,))],
        ),
        compiler_params=COPIES,
        cost_estimate=pl.CostEstimate(
            flops=0, bytes_accessed=4 * rows * columns, transcendentals=0
        ),
    )(target.reshape(1), out_proj)


def project_kernel(groups, *refs):
    ins, w_ref, out_ref = refs[:groups], refs[groups], refs[groups + 1]
    depth = ins[0].shape[1]
    columns = out_ref.shape[1]
    tile = columns // 4
    for i in range(4):
        at = slice(i * tile, (i + 1) * tile)
        acc = None
        for j in range(groups):
            row = pl.multiple_of(lax.bitwise_xor(my_group(), j) * depth, depth)
            dot = jnp.dot(
                ins[j][...], w_ref[pl.ds(row, depth), at], preferred_element_type=jnp.float32
            )
            acc = dot if acc is None else acc + dot
        out_ref[:, at] = acc.astype(out_ref.dtype)


def project(parts, held, dtype):
    groups = len(parts)
    half = parts[0].shape[0]
    rows, columns = held.shape
    return pl.pallas_call(
        functools.partial(project_kernel, groups),
        out_shape=jax.ShapeDtypeStruct((half, columns), dtype),
        in_specs=[VMEM] * (groups + 1),
        out_specs=VMEM,
        compiler_params=PARAMS,
        cost_estimate=pl.CostEstimate(
            flops=2 * half * rows * columns,
            bytes_accessed=2 * rows * columns,
            transcendentals=0,
        ),
    )(*parts, held)


def finish_kernel(groups, *refs):
    parts_ref, mine_ref, other_ref = refs[:3]
    sums, out_ref = refs[3:-1], refs[-1]
    width = mine_ref.shape[2]
    depth = parts_ref.shape[2]
    half = out_ref.shape[0] // 2
    core = lax.rem(lax.axis_index("ctx"), 2)
    group = my_group()
    for j in range(groups):
        for which, ref in ((core, mine_ref), (1 - core, other_ref)):
            at = (2 * lax.bitwise_xor(group, j) + which) * width
            at = pl.ds(pl.multiple_of(at, width), width)
            for i in range(2):
                acc = None
                for array in sums[i * (len(sums) // 2) : (i + 1) * (len(sums) // 2)]:
                    here = array[:, at].astype(jnp.float32)
                    acc = here if acc is None else acc + here
                for m in range(groups):
                    row = pl.multiple_of(lax.bitwise_xor(group, m) * depth, depth)
                    acc = acc + jnp.dot(
                        parts_ref[i * groups + m],
                        ref[j, pl.ds(row, depth), :],
                        preferred_element_type=jnp.float32,
                    )
                out_ref[i * half : (i + 1) * half, at] = acc.astype(out_ref.dtype)


def finish(parts, mine, other, low, high, groups):
    half, columns = low[0].shape
    return pl.pallas_call(
        functools.partial(finish_kernel, groups),
        out_shape=jax.ShapeDtypeStruct((2 * half, columns), jnp.bfloat16),
        in_specs=[VMEM] * (3 + len(low) + len(high)),
        out_specs=VMEM,
        name="finish",
        compiler_params=PARAMS,
        cost_estimate=pl.CostEstimate(
            flops=4 * half * mine.shape[1] * columns, bytes_accessed=12 << 20, transcendentals=0
        ),
    )(parts, mine, other, *low, *high)


def exchange_body(queries, attn_keys, attn_values, out_proj):
    ctx_count, tp_count = lax.axis_size("ctx"), lax.axis_size("tp")
    z = lax.axis_index("tp")
    groups = ctx_count // 2
    half = queries.shape[0] // 2
    width = queries.shape[1] // groups
    f32, bf16 = jnp.float32, jnp.bfloat16
    others = range(groups - 1, 0, -1)
    ends = [(0, 1), (tp_count - 1, tp_count - 2)]

    def swap(arrays):
        got = {0: arrays[0]}
        for j in others:
            pairs = [(d, d ^ (2 * j)) for d in range(ctx_count)]
            got[j] = lax.ppermute(arrays[j], "ctx", pairs)
        return [got[j] for j in range(groups)]

    def pair_swap(array):
        return lax.ppermute(array, "ctx", [(d, d ^ 1) for d in range(ctx_count)])

    def tokens(row0):
        packed = pack(queries, attn_keys, attn_values, row0, half, groups)
        return swap(packed)

    def paired(own):
        stacked = jnp.stack([array[1:] for array in own])
        return own, pair_swap(stacked)

    def attended(phase_inputs):
        outs = attention(phase_inputs, groups, half, width)
        return swap(outs)

    out_proj = pltpu.with_memory_space_constraint(out_proj, pltpu.HBM)
    queries = pltpu.with_memory_space_constraint(queries, pltpu.HBM)
    attn_keys = pltpu.with_memory_space_constraint(attn_keys, pltpu.HBM)
    attn_values = pltpu.with_memory_space_constraint(attn_values, pltpu.HBM)
    low = tokens(0)
    share = piece(out_proj, tp_count, ctx_count)
    share = lax.ppermute(share, "tp", ends)
    lower = z < tp_count // 2
    held = {}
    for t in range(tp_count - 1, tp_count // 2 - 1, -1):
        held[f"a{t}"] = jnp.where(lower, t, tp_count - 1 - t)
    for t in range(tp_count - 1, tp_count // 2, -1):
        held[f"b{t}"] = jnp.where(lower, tp_count - 1 - t, t)
    held["own"] = z
    for tag in held:
        held[tag] = hold(out_proj, held[tag].astype(jnp.int32), tp_count)

    low = paired(low)
    parts_low = attended([low])
    high = paired(tokens(half))
    parts_high = attended([low, high])

    share = swap([share] * groups)
    mine = jnp.stack(share)
    other = pair_swap(mine)

    def line(parts):
        chunks = {}
        for tag in held:
            chunks[tag] = project(parts, held[tag], f32)
        last = [chunks["own"]]
        for t in range(tp_count - 1, 1, -1):
            arrived = None
            for l in range(t):
                send = chunks[f"a{t}" if 2 * l < tp_count else f"b{t}"]
                if arrived is not None:
                    send = send + arrived.astype(f32)
                send = send.astype(bf16)
                pairs = [(l, l + 1), (tp_count - 1 - l, tp_count - 2 - l)]
                arrived = lax.ppermute(send, "tp", pairs)
            last.append(arrived)
        return last

    low_sums = line(parts_low)
    high_sums = line(parts_high)
    near = lax.ppermute(jnp.stack(parts_low + parts_high), "tp", ends)
    return finish(near, mine, other, low_sums, high_sums, groups)


def body(queries, attn_keys, attn_values, out_proj):
    ctx_count, tp_count = lax.axis_size("ctx"), lax.axis_size("tp")
    heads_local = queries.shape[1] // HS
    groups = ctx_count // 2
    paired = ctx_count % 2 == 0 and groups > 1 and groups & (groups - 1) == 0
    if paired and heads_local % groups == 0 and tp_count > 3 and tp_count % 2 == 0:
        return exchange_body(queries, attn_keys, attn_values, out_proj)
    return general_body(queries, attn_keys, attn_values, out_proj)


def solution(mesh):
    in_specs = (P("ctx", "tp"), P("ctx", "tp"), P("ctx", "tp"), P("tp", None))
    out_specs = P("ctx", "tp")
    return jax.shard_map(body, mesh=mesh, in_specs=in_specs, out_specs=out_specs, check_vma=False)
```

time: 200 us -> 186 us (0.930)
  starting transfers between devices: 0.08 us -> 36 us
  matrix products: 27.2 us -> 0 us
  Pallas kernels: 0 us -> 25.7 us
  waiting for transfers between devices: 139 us -> 119 us
  local copies, waits for them, and re-layouts: 14.7 us -> 0.12 us
  between operations: 13.2 us -> 0.48 us
    ppermute x0 -> x30, waiting for transfers between devices: none -> 119 us  [the longest x10 83.4 us: line(): arrived = lax.ppermute(send, 'tp', pairs)]
    reduce_scatter x1 -> x0, waiting for transfers between devices: 76.9 us -> none  [body(): lax.psum_scatter(partial_value.astype(jnp.float32).astype(jnp.bfloat16),...]
    all_gather x2 -> x0, waiting for transfers between devices: 61.5 us -> none  [the longest x1 39.4 us: body(): key_piece = lax.all_gather(attn_keys, 'ctx', axis=0, tiled=True)]
    ppermute x0 -> x30, starting transfers between devices: none -> 36 us  [the longest x15 18.1 us: swap(): got[j] = lax.ppermute(arrays[j], 'ctx', pairs)]
    dot_general x3 -> x0, matrix products: 27.2 us -> none  [the longest x1 12.1 us: body(): jnp.dot(attended, out_proj, preferred_element_type=jnp.float32)]
    pallas_call x0 -> x18, Pallas kernels: none -> 25.7 us  [the longest x4 9.14 us: hold(): pl.pallas_call(hold_kernel, out_shape=jax.ShapeDtypeStruct((rows, columns...]
    unnamed x5 -> x7, local copies, waits for them, and re-layouts: 8.17 us -> 0.04 us
    all_gather x1 -> x0, local copies, waits for them, and re-layouts: 6.52 us -> none  [body(): value_piece = lax.all_gather(attn_values, 'ctx', axis=0, tiled=True)]
  transfers between devices with their start and end apart: 3 -> 30, of which waited for: 3 -> 14; matrix products, arithmetic and copies ran while one was open for 5% -> 2% of each run, Pallas kernels for 0% -> 12%
where the time goes in v1:
time: 186 us; the launch traced here: 185 us
  waiting for transfers between devices  119 us (64%)
  starting transfers between devices  36 us (19%)
  Pallas kernels  25.7 us (14%)
  other arithmetic  3.93 us (2%)
    ppermute x10, waiting for transfers between devices, line(): arrived = lax.ppermute(send, 'tp', pairs)  83.4 us
    ppermute x15, waiting for transfers between devices, swap(): got[j] = lax.ppermute(arrays[j], 'ctx', pairs)  35.8 us
    ppermute x15, starting transfers between devices, swap(): got[j] = lax.ppermute(arrays[j], 'ctx', pairs)  18.1 us
    ppermute x10, starting transfers between devices, line(): arrived = lax.ppermute(send, 'tp', pairs)  10.6 us
    pallas_call x4, Pallas kernels, hold(): pl.pallas_call(hold_kernel, out_shape=jax.ShapeDtypeStruct((rows, columns...  9.14 us
    pallas_call x8, Pallas kernels, project(): pl.pallas_call(functools.partial(project_kernel, groups), out_shape=jax.S...  5.88 us
    ppermute x1, starting transfers between devices, exchange_body(): share = lax.ppermute(share, 'tp', ends)  5.75 us
    pallas_call x2, Pallas kernels, attention(): pl.pallas_call(functools.partial(attention_kernel, groups, phases), out_s...  4.75 us
  transfers between devices with their start and end apart: 30, of which 14 were waited for; matrix products, arithmetic and copies ran while one was open for 2% of the time, Pallas kernels for 12%

profile of v1, /device:TPU:0, one launch (start us, length us, event | category | flops | bytes accessed | tf_op | source)
XLA Modules:
  0.0 185.4 jit_solution(10146580539408289434)
XLA Ops:
  0.0 1.0 piece.1
  1.1 5.8 %collective-permute-start.15 = (bf16[1024,256]{1,0:T(8,128)(2,1)S(1)}, bf16[1024,256]{1,0:T(8,128)(2,1)}, u32[]{:S(2)}, u32[]{:S(2)}) collective-permute-start(bf16[1024,256]{1,0:T(8,128)(2,1)S(1)} %piece.1), channel_id=1, source_target_pairs={{0,1},{3,2},{4,5},{7,6},{8,9},{11,10},{12,13},{15,14},{16,17},{19,... | collective-permute-start | bytes 1572872 | tf_op jit(solution)/shard_map/ppermute | solution.py:368
  6.8 1.3 shard_map.48
  8.1 1.6 collective-permute-start.7
  9.6 1.5 collective-permute-start.8
  11.2 0.5 collective-permute-start.9
  11.6 1.3 shard_map.46
  12.9 1.6 collective-permute-start
  14.5 1.4 collective-permute-done.7.refs_6_
  15.9 1.5 collective-permute-start.1
  17.5 2.9 %collective-permute-done.8.refs_7_ = bf16[3,128,256]{2,1,0:T(8,128)(2,1)S(1)} collective-permute-done((bf16[3,128,256]{2,1,0:T(8,128)(2,1)S(1)}, bf16[3,128,256]{2,1,0:T(8,128)(2,1)S(1)}, u32[]{:S(2)}, u32[]{:S(2)}) %collective-permute-start.8) | collective-permute-done | bytes 196640 | tf_op jit(solution)/shard_map/ppermute | solution.py:344
  20.3 0.6 collective-permute-start.2
  21.0 0.2 collective-permute-done.9.refs_8_
  21.2 0.9 pad_maximum_fusion.2
  22.0 2.4 %collective-permute-done.refs_1_ = bf16[3,128,256]{2,1,0:T(8,128)(2,1)S(1)} collective-permute-done((bf16[3,128,256]{2,1,0:T(8,128)(2,1)S(1)}, bf16[3,128,256]{2,1,0:T(8,128)(2,1)S(1)}, u32[]{:S(2)}, u32[]{:S(2)}) %collective-permute-start) | collective-permute-done | bytes 196640 | tf_op jit(solution)/shard_map/ppermute | solution.py:344
  24.4 4.0 %collective-permute-done.1.refs_2_ = bf16[3,128,256]{2,1,0:T(8,128)(2,1)S(1)} collective-permute-done((bf16[3,128,256]{2,1,0:T(8,128)(2,1)S(1)}, bf16[3,128,256]{2,1,0:T(8,128)(2,1)S(1)}, u32[]{:S(2)}, u32[]{:S(2)}) %collective-permute-start.1) | collective-permute-done | bytes 196640 | tf_op jit(solution)/shard_map/ppermute | solution.py:344
  28.4 0.9 pad_maximum_fusion.1
  29.3 2.3 %shard_map.52.refs_4_ = bf16[1024,2048]{1,0:T(8,128)(2,1)S(1)} custom-call(s32[1]{0:T(128)} %bitcast.21.place_ref, bf16[1024,8192]{1,0:T(8,128)(2,1)} %w_ref.9), custom_call_target="tpu_custom_call" | custom-call | bytes 8388608 | tf_op jit(solution)/shard_map/pallas_call | solution.py:236
  31.6 2.3 %shard_map.56.refs_4_ = bf16[1024,2048]{1,0:T(8,128)(2,1)S(1)} custom-call(s32[1]{0:T(128)} %bitcast.23.place_ref, bf16[1024,8192]{1,0:T(8,128)(2,1)} %w_ref.9), custom_call_target="tpu_custom_call" | custom-call | bytes 8388608 | tf_op jit(solution)/shard_map/pallas_call | solution.py:236
  33.9 2.3 %shard_map.54.refs_4_ = bf16[1024,2048]{1,0:T(8,128)(2,1)S(1)} custom-call(s32[1]{0:T(128)} %bitcast.22.place_ref, bf16[1024,8192]{1,0:T(8,128)(2,1)} %w_ref.9), custom_call_target="tpu_custom_call" | custom-call | bytes 8388608 | tf_op jit(solution)/shard_map/pallas_call | solution.py:236
  36.2 1.6 collective-permute-start.18
  37.7 1.2 collective-permute-start.17
  38.9 3.4 %shard_map.49 = (bf16[128,256]{1,0:T(8,128)(2,1)S(1)}, bf16[128,256]{1,0:T(8,128)(2,1)S(1)}, bf16[128,256]{1,0:T(8,128)(2,1)S(1)}, bf16[128,256]{1,0:T(8,128)(2,1)S(1)}) custom-call(bf16[3,128,256]{2,1,0:T(8,128)(2,1)S(1)} %get-tuple-element.21.refs_0_, bf16[3,128,256]{2,1,0:T(8,128)(2,1)S(1)} %collective-permute-done.refs_1_, ...), custom_call_target="tpu_custom_call" | custom-call | flops 872415232 | bytes 2097152 | tf_op jit(solution)/shard_map/pallas_call | solution.py:211
  42.4 0.8 collective-permute-start.11
  43.2 1.3 collective-permute-start.12
  44.5 1.3 shard_map.47
  45.9 0.8 collective-permute-start.4
  46.7 7.9 %collective-permute-done.4.refs_1_ = bf16[128,256]{1,0:T(8,128)(2,1)S(1)} collective-permute-done((bf16[128,256]{1,0:T(8,128)(2,1)S(1)}, bf16[128,256]{1,0:T(8,128)(2,1)S(1)}, u32[]{:S(2)}, u32[]{:S(2)}) %collective-permute-start.4) | collective-permute-done | bytes 65568 | tf_op jit(solution)/shard_map/ppermute | solution.py:344
  54.6 0.5 collective-permute-start.5
  55.1 10.6 %collective-permute-done.5.refs_2_ = bf16[128,256]{1,0:T(8,128)(2,1)S(1)} collective-permute-done((bf16[128,256]{1,0:T(8,128)(2,1)S(1)}, bf16[128,256]{1,0:T(8,128)(2,1)S(1)}, u32[]{:S(2)}, u32[]{:S(2)}) %collective-permute-start.5) | collective-permute-done | bytes 65568 | tf_op jit(solution)/shard_map/ppermute | solution.py:344
  65.7 1.5 collective-permute-start.6
  67.2 3.7 %collective-permute-done.6.refs_3_ = bf16[128,256]{1,0:T(8,128)(2,1)S(1)} collective-permute-done((bf16[128,256]{1,0:T(8,128)(2,1)S(1)}, bf16[128,256]{1,0:T(8,128)(2,1)S(1)}, u32[]{:S(2)}, u32[]{:S(2)}) %collective-permute-start.6) | collective-permute-done | bytes 65568 | tf_op jit(solution)/shard_map/ppermute | solution.py:344
  70.9 1.5 collective-permute-start.13
  72.4 1.6 collective-permute-start.16
  74.0 2.8 %collective-permute-done.13.refs_3_ = bf16[128,256]{1,0:T(8,128)(2,1)S(1)} collective-permute-done((bf16[128,256]{1,0:T(8,128)(2,1)S(1)}, bf16[128,256]{1,0:T(8,128)(2,1)S(1)}, u32[]{:S(2)}, u32[]{:S(2)}) %collective-permute-start.13) | collective-permute-done | bytes 65568 | tf_op jit(solution)/shard_map/ppermute | solution.py:344
  76.7 0.7 shard_map.61
  77.5 1.3 collective-permute-start.28
  78.9 1.5 collective-permute-start.14
  80.5 0.7 shard_map.57
  81.3 0.7 shard_map.55
  82.1 0.7 shard_map.60
  82.9 0.7 shard_map.59
  83.7 0.7 shard_map.53
  84.4 1.3 collective-permute-start.23
  85.8 1.3 collective-permute-start.25
  87.1 1.3 collective-permute-start.20
  88.4 1.3 pad_maximum_fusion.refs_1_
  89.7 1.4 collective-permute-done.28
  91.3 33.6 %collective-permute-done.25 = bf16[128,2048]{1,0:T(8,128)(2,1)S(1)} collective-permute-done((bf16[128,2048]{1,0:T(8,128)(2,1)S(1)}, bf16[128,2048]{1,0:T(8,128)(2,1)S(1)}, u32[]{:S(2)}, u32[]{:S(2)}) %collective-permute-start.25) | collective-permute-done | bytes 524320 | tf_op jit(solution)/shard_map/ppermute | solution.py:401
  124.8 0.7 collective-permute-start.29
  125.5 0.1 add_convert_fusion.2
  125.6 6.8 %collective-permute-done.20 = bf16[128,2048]{1,0:T(8,128)(2,1)S(1)} collective-permute-done((bf16[128,2048]{1,0:T(8,128)(2,1)S(1)}, bf16[128,2048]{1,0:T(8,128)(2,1)S(1)}, u32[]{:S(2)}, u32[]{:S(2)}) %collective-permute-start.20) | collective-permute-done | bytes 524320 | tf_op jit(solution)/shard_map/ppermute | solution.py:401
  132.4 0.7 collective-permute-start.26
  133.1 0.1 add_convert_fusion.5
  133.3 0.7 collective-permute-start.21
  134.1 0.7 collective-permute-start.24
  134.9 1.3 collective-permute-start.27
  136.3 1.3 collective-permute-start.22
  137.6 2.3 %shard_map.50.refs_4_ = bf16[1024,2048]{1,0:T(8,128)(2,1)S(1)} custom-call(s32[1]{0:T(128)} %bitcast.20.place_ref, bf16[1024,8192]{1,0:T(8,128)(2,1)} %w_ref.9), custom_call_target="tpu_custom_call" | custom-call | bytes 8388608 | tf_op jit(solution)/shard_map/pallas_call | solution.py:236
  139.9 0.7 shard_map.58.refs_6_
  140.7 0.7 shard_map.51.refs_3_
  141.4 36.0 %collective-permute-done.27.refs_7_ = bf16[128,2048]{1,0:T(8,128)(2,1)S(1)} collective-permute-done((bf16[128,2048]{1,0:T(8,128)(2,1)S(1)}, bf16[128,2048]{1,0:T(8,128)(2,1)S(1)}, u32[]{:S(2)}, u32[]{:S(2)}) %collective-permute-start.27) | collective-permute-done | bytes 524320 | tf_op jit(solution)/shard_map/ppermute | solution.py:401
  177.4 5.6 %collective-permute-done.22.refs_4_ = bf16[128,2048]{1,0:T(8,128)(2,1)S(1)} collective-permute-done((bf16[128,2048]{1,0:T(8,128)(2,1)S(1)}, bf16[128,2048]{1,0:T(8,128)(2,1)S(1)}, u32[]{:S(2)}, u32[]{:S(2)}) %collective-permute-start.22) | collective-permute-done | bytes 524320 | tf_op jit(solution)/shard_map/ppermute | solution.py:401
  183.0 2.4 %finish.1 = bf16[256,2048]{1,0:T(8,128)(2,1)} custom-call(bf16[8,128,256]{2,1,0:T(8,128)(2,1)S(1)} %collective-permute-done.14.refs_0_, bf16[4,1024,256]{2,1,0:T(8,128)(2,1)S(1)} %pad_maximum_fusion.refs_1_, bf16[4,1024,256]{2,1,0:T(8,128)(2,1)S(1)} %collective-permute-done.19.refs_2_, f32[128,2048]{1,0:T(8,128)S(1)} %shard_map.51.refs_3_, ...), custom_call_target="tpu_custom_call" | custom-call | flops 1073741824 | bytes 12582912 | tf_op jit(solution)/shard_map/finish/pallas_call | solution.py:317
  (43 shorter events, 0.8 us)
Async XLA Ops:
  1.1 35.1 %collective-permute-start.15 = (bf16[1024,256]{1,0:T(8,128)(2,1)S(1)}, bf16[1024,256]{1,0:T(8,128)(2,1)}, u32[]{:S(2)}, u32[]{:S(2)}) collective-permute-start(bf16[1024,256]{1,0:T(8,128)(2,1)S(1)} %piece.1), channel_id=1, source_target_pairs={{0,1},{3,2},{4,5},{7,6},{8,9},{11,10},{12,13},{15,14},{16,17},{19,... | collective-permute-start | bytes 1572872 | tf_op jit(solution)/shard_map/ppermute | solution.py:368
  8.1 7.8 %collective-permute-start.7 = (bf16[3,128,256]{2,1,0:T(8,128)(2,1)S(1)}, bf16[3,128,256]{2,1,0:T(8,128)(2,1)S(1)}, u32[]{:S(2)}, u32[]{:S(2)}) collective-permute-start(bf16[3,128,256]{2,1,0:T(8,128)(2,1)S(1)} %get-tuple-element.30), channel_id=1, source_target_pairs={{0,8},{4,12},{8,0},{12,4},{16,24},{20,28},{24,16},{28,20},{1,9},{5... | collective-permute-start | bytes 589832 | tf_op jit(solution)/shard_map/ppermute | solution.py:344
  9.6 10.7 %collective-permute-start.8 = (bf16[3,128,256]{2,1,0:T(8,128)(2,1)S(1)}, bf16[3,128,256]{2,1,0:T(8,128)(2,1)S(1)}, u32[]{:S(2)}, u32[]{:S(2)}) collective-permute-start(bf16[3,128,256]{2,1,0:T(8,128)(2,1)S(1)} %get-tuple-element.31), channel_id=1, source_target_pairs={{0,16},{4,20},{8,24},{12,28},{16,0},{20,4},{24,8},{28,12},{1,17},{... | collective-permute-start | bytes 589832 | tf_op jit(solution)/shard_map/ppermute | solution.py:344
  11.2 10.0 %collective-permute-start.9 = (bf16[3,128,256]{2,1,0:T(8,128)(2,1)S(1)}, bf16[3,128,256]{2,1,0:T(8,128)(2,1)S(1)}, u32[]{:S(2)}, u32[]{:S(2)}) collective-permute-start(bf16[3,128,256]{2,1,0:T(8,128)(2,1)S(1)} %get-tuple-element.32), channel_id=1, source_target_pairs={{0,24},{4,28},{8,16},{12,20},{16,8},{20,12},{24,0},{28,4},{1,25},{... | collective-permute-start | bytes 589832 | tf_op jit(solution)/shard_map/ppermute | solution.py:344
  12.9 11.5 %collective-permute-start = (bf16[3,128,256]{2,1,0:T(8,128)(2,1)S(1)}, bf16[3,128,256]{2,1,0:T(8,128)(2,1)S(1)}, u32[]{:S(2)}, u32[]{:S(2)}) collective-permute-start(bf16[3,128,256]{2,1,0:T(8,128)(2,1)S(1)} %get-tuple-element.22), channel_id=1, source_target_pairs={{0,8},{4,12},{8,0},{12,4},{16,24},{20,28},{24,16},{28,20},{1,9},{5... | collective-permute-start | bytes 589832 | tf_op jit(solution)/shard_map/ppermute | solution.py:344
  15.9 12.4 %collective-permute-start.1 = (bf16[3,128,256]{2,1,0:T(8,128)(2,1)S(1)}, bf16[3,128,256]{2,1,0:T(8,128)(2,1)S(1)}, u32[]{:S(2)}, u32[]{:S(2)}) collective-permute-start(bf16[3,128,256]{2,1,0:T(8,128)(2,1)S(1)} %get-tuple-element.23), channel_id=1, source_target_pairs={{0,16},{4,20},{8,24},{12,28},{16,0},{20,4},{24,8},{28,12},{1,17},{... | collective-permute-start | bytes 589832 | tf_op jit(solution)/shard_map/ppermute | solution.py:344
  20.3 8.1 %collective-permute-start.2 = (bf16[3,128,256]{2,1,0:T(8,128)(2,1)S(1)}, bf16[3,128,256]{2,1,0:T(8,128)(2,1)S(1)}, u32[]{:S(2)}, u32[]{:S(2)}) collective-permute-start(bf16[3,128,256]{2,1,0:T(8,128)(2,1)S(1)} %get-tuple-element.24), channel_id=1, source_target_pairs={{0,24},{4,28},{8,16},{12,20},{16,8},{20,12},{24,0},{28,4},{1,25},{... | collective-permute-start | bytes 589832 | tf_op jit(solution)/shard_map/ppermute | solution.py:344
  22.0 16.9 %collective-permute-start.10 = (bf16[4,2,128,256]{3,2,1,0:T(8,128)(2,1)}, bf16[4,2,128,256]{3,2,1,0:T(8,128)(2,1)S(1)}, u32[]{:S(2)}, u32[]{:S(2)}) collective-permute-start(bf16[4,2,128,256]{3,2,1,0:T(8,128)(2,1)} %pad_maximum_fusion.2), channel_id=1, source_target_pairs={{0,4},{4,0},{8,12},{12,8},{16,20},{20,16},{24,28},{28,24},{1,5},{5... | collective-permute-start | bytes 1572872 | tf_op jit(solution)/shard_map/ppermute | solution.py:348
  29.3 9.7 %collective-permute-start.3 = (bf16[4,2,128,256]{3,2,1,0:T(8,128)(2,1)}, bf16[4,2,128,256]{3,2,1,0:T(8,128)(2,1)S(1)}, u32[]{:S(2)}, u32[]{:S(2)}) collective-permute-start(bf16[4,2,128,256]{3,2,1,0:T(8,128)(2,1)} %pad_maximum_fusion.1), channel_id=1, source_target_pairs={{0,4},{4,0},{8,12},{12,8},{16,20},{20,16},{24,28},{28,24},{1,5},{5... | collective-permute-start | bytes 1572872 | tf_op jit(solution)/shard_map/ppermute | solution.py:348
  36.2 48.3 %collective-permute-start.18 = (bf16[1024,256]{1,0:T(8,128)(2,1)}, bf16[1024,256]{1,0:T(8,128)(2,1)S(1)}, u32[]{:S(2)}, u32[]{:S(2)}) collective-permute-start(bf16[1024,256]{1,0:T(8,128)(2,1)} %collective-permute-done.15), channel_id=1, source_target_pairs={{0,24},{4,28},{8,16},{12,20},{16,8},{20,12},{24,0},{28,4},{1,25},{... | collective-permute-start | bytes 1572872 | tf_op jit(solution)/shard_map/ppermute | solution.py:344
  37.7 48.0 %collective-permute-start.17 = (bf16[1024,256]{1,0:T(8,128)(2,1)}, bf16[1024,256]{1,0:T(8,128)(2,1)S(1)}, u32[]{:S(2)}, u32[]{:S(2)}) collective-permute-start(bf16[1024,256]{1,0:T(8,128)(2,1)} %collective-permute-done.15), channel_id=1, source_target_pairs={{0,16},{4,20},{8,24},{12,28},{16,0},{20,4},{24,8},{28,12},{1,17},{... | collective-permute-start | bytes 1572872 | tf_op jit(solution)/shard_map/ppermute | solution.py:344
  42.4 30.0 %collective-permute-start.11 = (bf16[128,256]{1,0:T(8,128)(2,1)S(1)}, bf16[128,256]{1,0:T(8,128)(2,1)S(1)}, u32[]{:S(2)}, u32[]{:S(2)}) collective-permute-start(bf16[128,256]{1,0:T(8,128)(2,1)S(1)} %get-tuple-element.34), channel_id=1, source_target_pairs={{0,8},{4,12},{8,0},{12,4},{16,24},{20,28},{24,16},{28,20},{1,9},{5... | collective-permute-start | bytes 196616 | tf_op jit(solution)/shard_map/ppermute | solution.py:344
  43.2 30.8 %collective-permute-start.12 = (bf16[128,256]{1,0:T(8,128)(2,1)S(1)}, bf16[128,256]{1,0:T(8,128)(2,1)S(1)}, u32[]{:S(2)}, u32[]{:S(2)}) collective-permute-start(bf16[128,256]{1,0:T(8,128)(2,1)S(1)} %get-tuple-element.35), channel_id=1, source_target_pairs={{0,16},{4,20},{8,24},{12,28},{16,0},{20,4},{24,8},{28,12},{1,17},{... | collective-permute-start | bytes 196616 | tf_op jit(solution)/shard_map/ppermute | solution.py:344
  45.9 8.7 %collective-permute-start.4 = (bf16[128,256]{1,0:T(8,128)(2,1)S(1)}, bf16[128,256]{1,0:T(8,128)(2,1)S(1)}, u32[]{:S(2)}, u32[]{:S(2)}) collective-permute-start(bf16[128,256]{1,0:T(8,128)(2,1)S(1)} %get-tuple-element.26), channel_id=1, source_target_pairs={{0,8},{4,12},{8,0},{12,4},{16,24},{20,28},{24,16},{28,20},{1,9},{5... | collective-permute-start | bytes 196616 | tf_op jit(solution)/shard_map/ppermute | solution.py:344
  54.6 11.1 %collective-permute-start.5 = (bf16[128,256]{1,0:T(8,128)(2,1)S(1)}, bf16[128,256]{1,0:T(8,128)(2,1)S(1)}, u32[]{:S(2)}, u32[]{:S(2)}) collective-permute-start(bf16[128,256]{1,0:T(8,128)(2,1)S(1)} %get-tuple-element.27), channel_id=1, source_target_pairs={{0,16},{4,20},{8,24},{12,28},{16,0},{20,4},{24,8},{28,12},{1,17},{... | collective-permute-start | bytes 196616 | tf_op jit(solution)/shard_map/ppermute | solution.py:344
  65.7 5.2 %collective-permute-start.6 = (bf16[128,256]{1,0:T(8,128)(2,1)S(1)}, bf16[128,256]{1,0:T(8,128)(2,1)S(1)}, u32[]{:S(2)}, u32[]{:S(2)}) collective-permute-start(bf16[128,256]{1,0:T(8,128)(2,1)S(1)} %get-tuple-element.28), channel_id=1, source_target_pairs={{0,24},{4,28},{8,16},{12,20},{16,8},{20,12},{24,0},{28,4},{1,25},{... | collective-permute-start | bytes 196616 | tf_op jit(solution)/shard_map/ppermute | solution.py:344
  70.9 5.9 %collective-permute-start.13 = (bf16[128,256]{1,0:T(8,128)(2,1)S(1)}, bf16[128,256]{1,0:T(8,128)(2,1)S(1)}, u32[]{:S(2)}, u32[]{:S(2)}) collective-permute-start(bf16[128,256]{1,0:T(8,128)(2,1)S(1)} %get-tuple-element.36), channel_id=1, source_target_pairs={{0,24},{4,28},{8,16},{12,20},{16,8},{20,12},{24,0},{28,4},{1,25},{... | collective-permute-start | bytes 196616 | tf_op jit(solution)/shard_map/ppermute | solution.py:344
  72.4 14.7 %collective-permute-start.16 = (bf16[1024,256]{1,0:T(8,128)(2,1)}, bf16[1024,256]{1,0:T(8,128)(2,1)S(1)}, u32[]{:S(2)}, u32[]{:S(2)}) collective-permute-start(bf16[1024,256]{1,0:T(8,128)(2,1)} %collective-permute-done.15), channel_id=1, source_target_pairs={{0,8},{4,12},{8,0},{12,4},{16,24},{20,28},{24,16},{28,20},{1,9},{5... | collective-permute-start | bytes 1572872 | tf_op jit(solution)/shard_map/ppermute | solution.py:344
  77.5 13.6 %collective-permute-start.28 = (bf16[128,2048]{1,0:T(8,128)(2,1)S(1)}, bf16[128,2048]{1,0:T(8,128)(2,1)S(1)}, u32[]{:S(2)}, u32[]{:S(2)}) collective-permute-start(bf16[128,2048]{1,0:T(8,128)(2,1)S(1)} %convert_element_type.61), channel_id=1, source_target_pairs={{0,1},{3,2},{4,5},{7,6},{8,9},{11,10},{12,13},{15,14},{16,17},{19,... | collective-permute-start | bytes 1572872 | tf_op jit(solution)/shard_map/ppermute | solution.py:401
  78.9 57.4 %collective-permute-start.14 = (bf16[8,128,256]{2,1,0:T(8,128)(2,1)S(1)}, bf16[8,128,256]{2,1,0:T(8,128)(2,1)S(1)}, u32[]{:S(2)}, u32[]{:S(2)}) collective-permute-start(bf16[8,128,256]{2,1,0:T(8,128)(2,1)S(1)} %bitcast_dynamic-update-slice_fusion), channel_id=1, source_target_pairs={{0,1},{3,2},{4,5},{7,6},{8,9},{11,10},{12,13},{15,14},{16,17},{19,... | collective-permute-start | bytes 1572872 | tf_op jit(solution)/shard_map/ppermute | solution.py:407
  84.4 48.8 %collective-permute-start.23 = (bf16[128,2048]{1,0:T(8,128)(2,1)S(1)}, bf16[128,2048]{1,0:T(8,128)(2,1)S(1)}, u32[]{:S(2)}, u32[]{:S(2)}) collective-permute-start(bf16[128,2048]{1,0:T(8,128)(2,1)S(1)} %convert_element_type.53), channel_id=1, source_target_pairs={{0,1},{3,2},{4,5},{7,6},{8,9},{11,10},{12,13},{15,14},{16,17},{19,... | collective-permute-start | bytes 1572872 | tf_op jit(solution)/shard_map/ppermute | solution.py:401
  85.8 39.1 %collective-permute-start.25 = (bf16[128,2048]{1,0:T(8,128)(2,1)S(1)}, bf16[128,2048]{1,0:T(8,128)(2,1)S(1)}, u32[]{:S(2)}, u32[]{:S(2)}) collective-permute-start(bf16[128,2048]{1,0:T(8,128)(2,1)S(1)} %convert_element_type.56), channel_id=1, source_target_pairs={{0,1},{3,2},{4,5},{7,6},{8,9},{11,10},{12,13},{15,14},{16,17},{19,... | collective-permute-start | bytes 1572872 | tf_op jit(solution)/shard_map/ppermute | solution.py:401
  87.1 45.3 %collective-permute-start.20 = (bf16[128,2048]{1,0:T(8,128)(2,1)S(1)}, bf16[128,2048]{1,0:T(8,128)(2,1)S(1)}, u32[]{:S(2)}, u32[]{:S(2)}) collective-permute-start(bf16[128,2048]{1,0:T(8,128)(2,1)S(1)} %convert_element_type.48), channel_id=1, source_target_pairs={{0,1},{3,2},{4,5},{7,6},{8,9},{11,10},{12,13},{15,14},{16,17},{19,... | collective-permute-start | bytes 1572872 | tf_op jit(solution)/shard_map/ppermute | solution.py:401
  91.1 91.9 %collective-permute-start.19 = (bf16[4,1024,256]{2,1,0:T(8,128)(2,1)S(1)}, bf16[4,1024,256]{2,1,0:T(8,128)(2,1)S(1)}, u32[]{:S(2)}, u32[]{:S(2)}) collective-permute-start(bf16[4,1024,256]{2,1,0:T(8,128)(2,1)S(1)} %pad_maximum_fusion.refs_1_), channel_id=1, source_target_pairs={{0,4},{4,0},{8,12},{12,8},{16,20},{20,16},{24,28},{28,24},{1,5},{5... | collective-permute-start | bytes 6291464 | tf_op jit(solution)/shard_map/ppermute | solution.py:348
  124.8 16.6 %collective-permute-start.29 = (bf16[128,2048]{1,0:T(8,128)(2,1)S(1)}, bf16[128,2048]{1,0:T(8,128)(2,1)S(1)}, u32[]{:S(2)}, u32[]{:S(2)}) collective-permute-start(bf16[128,2048]{1,0:T(8,128)(2,1)S(1)} %add_convert_fusion), channel_id=1, source_target_pairs={{1,2},{2,1},{5,6},{6,5},{9,10},{10,9},{13,14},{14,13},{17,18},{18,... | collective-permute-start | bytes 1572872 | tf_op jit(solution)/shard_map/ppermute | solution.py:401
  132.4 1.6 collective-permute-start.26
  133.3 1.6 collective-permute-start.21
  134.1 7.3 %collective-permute-start.24 = (bf16[128,2048]{1,0:T(8,128)(2,1)S(1)}, bf16[128,2048]{1,0:T(8,128)(2,1)S(1)}, u32[]{:S(2)}, u32[]{:S(2)}) collective-permute-start(bf16[128,2048]{1,0:T(8,128)(2,1)S(1)} %add_convert_fusion.3), channel_id=1, source_target_pairs={{1,2},{2,1},{5,6},{6,5},{9,10},{10,9},{13,14},{14,13},{17,18},{18,... | collective-permute-start | bytes 1572872 | tf_op jit(solution)/shard_map/ppermute | solution.py:401
  134.9 42.5 %collective-permute-start.27 = (bf16[128,2048]{1,0:T(8,128)(2,1)S(1)}, bf16[128,2048]{1,0:T(8,128)(2,1)S(1)}, u32[]{:S(2)}, u32[]{:S(2)}) collective-permute-start(bf16[128,2048]{1,0:T(8,128)(2,1)S(1)} %add_convert_fusion.1), channel_id=1, source_target_pairs={{2,3},{1,0},{6,7},{5,4},{10,11},{9,8},{14,15},{13,12},{18,19},{17,... | collective-permute-start | bytes 1572872 | tf_op jit(solution)/shard_map/ppermute | solution.py:401
  136.3 46.7 %collective-permute-start.22 = (bf16[128,2048]{1,0:T(8,128)(2,1)S(1)}, bf16[128,2048]{1,0:T(8,128)(2,1)S(1)}, u32[]{:S(2)}, u32[]{:S(2)}) collective-permute-start(bf16[128,2048]{1,0:T(8,128)(2,1)S(1)} %add_convert_fusion.4), channel_id=1, source_target_pairs={{2,3},{1,0},{6,7},{5,4},{10,11},{9,8},{14,15},{13,12},{18,19},{17,... | collective-permute-start | bytes 1572872 | tf_op jit(solution)/shard_map/ppermute | solution.py:401

commit v2 on v1

--- a/solution.py
+++ b/solution.py
@@ -127,7 +127,7 @@
 def attend(groups, phases, group, core, ins, outs):
     half, width = outs[0].shape
     rate = math.log2(math.e) / HS**0.5
-    per_phase = groups + 1
+    per_phase = 2 * groups
     row = lax.broadcasted_iota(jnp.int32, (half, 2 * half), 0)
     col = lax.broadcasted_iota(jnp.int32, (half, 2 * half), 1)
     other_seen = core == (1 if phases == 1 else 0)
@@ -148,10 +148,8 @@
 
     def keys_of(phase, at, which, lanes):
         own = ins[phase * per_phase + (at ^ group)]
-        other = ins[phase * per_phase + groups]
-        return jnp.concatenate(
-            [own[which, :, lanes], other[at ^ group, which - 1, :, lanes]], axis=0
-        )
+        other = ins[phase * per_phase + groups + (at ^ group)]
+        return jnp.concatenate([own[which, :, lanes], other[which, :, lanes]], axis=0)
 
     def rows(array, i):
         return array[i * half : (i + 1) * half]
@@ -205,7 +203,7 @@
 
 def attention(phase_inputs, groups, half, width):
     phases = len(phase_inputs)
-    flat = [array for own, other in phase_inputs for array in (*own, other)]
+    flat = [array for own, other in phase_inputs for array in (*own, *other)]
     out = jax.ShapeDtypeStruct((half, width), jnp.bfloat16)
     elements = groups * width // HS * half * half * (groups + 1 if phases == 1 else 3 * groups + 1)
     return pl.pallas_call(
@@ -285,46 +283,88 @@
     )(*parts, held)
 
 
-def finish_kernel(groups, *refs):
-    parts_ref, mine_ref, other_ref = refs[:3]
-    sums, out_ref = refs[3:-1], refs[-1]
-    width = mine_ref.shape[2]
+def near_kernel(groups, *refs):
+    parts_ref, mine, other = refs[0], refs[1 : groups + 1], refs[groups + 1 : 2 * groups + 1]
+    sums, outs = refs[2 * groups + 1 : -2], refs[-2:]
+    width = mine[0].shape[1]
     depth = parts_ref.shape[2]
-    half = out_ref.shape[0] // 2
     core = lax.rem(lax.axis_index("ctx"), 2)
     group = my_group()
     for j in range(groups):
-        for which, ref in ((core, mine_ref), (1 - core, other_ref)):
+        for which, ref in ((core, mine[j]), (1 - core, other[j])):
             at = (2 * lax.bitwise_xor(group, j) + which) * width
             at = pl.ds(pl.multiple_of(at, width), width)
-            for i in range(2):
-                acc = None
-                for array in sums[i * (len(sums) // 2) : (i + 1) * (len(sums) // 2)]:
-                    here = array[:, at].astype(jnp.float32)
-                    acc = here if acc is None else acc + here
+            for i, out_ref in enumerate(outs):
+                acc = sums[i][:, at].astype(jnp.float32)
+                for array in sums[2:] if i == 0 else ():
+                    acc = acc + array[:, at].astype(jnp.float32)
                 for m in range(groups):
                     row = pl.multiple_of(lax.bitwise_xor(group, m) * depth, depth)
                     acc = acc + jnp.dot(
                         parts_ref[i * groups + m],
-                        ref[j, pl.ds(row, depth), :],
+                        ref[pl.ds(row, depth), :],
                         preferred_element_type=jnp.float32,
                     )
-                out_ref[i * half : (i + 1) * half, at] = acc.astype(out_ref.dtype)
-
-
-def finish(parts, mine, other, low, high, groups):
+                out_ref[:, at] = acc.astype(out_ref.dtype)
+
+
+def near_sums(parts, mine, other, low, high, groups):
     half, columns = low[0].shape
     return pl.pallas_call(
-        functools.partial(finish_kernel, groups),
+        functools.partial(near_kernel, groups),
+        out_shape=[
+            jax.ShapeDtypeStruct((half, columns), jnp.bfloat16),
+            jax.ShapeDtypeStruct((half, columns), jnp.float32),
+        ],
+        in_specs=[VMEM] * (2 * groups + 2 + len(low)),
+        out_specs=[VMEM] * 2,
+        name="nsum",
+        compiler_params=PARAMS,
+        cost_estimate=pl.CostEstimate(
+            flops=4 * half * mine[0].shape[0] * columns, bytes_accessed=12 << 20, transcendentals=0
+        ),
+    )(parts, *mine, *other, low[0], high, *low[1:])
+
+
+def finish_kernel(low_ref, high_ref, *refs):
+    arrived, out_ref, made, sems = refs[:-3], refs[-3], refs[-2], refs[-1]
+    half, columns = made.shape
+    count = sems.shape[0] - 1
+    tile = columns // count
+    copies = [pltpu.make_async_copy(low_ref, out_ref.at[pl.ds(0, half), :], sems.at[count])]
+    copies[0].start()
+    for i in range(count):
+        at = pl.ds(i * tile, tile)
+        acc = high_ref[:, at]
+        for ref in arrived:
+            acc = acc + ref[:, at].astype(jnp.float32)
+        made[:, at] = acc.astype(made.dtype)
+        copy = pltpu.make_async_copy(
+            made.at[:, at], out_ref.at[pl.ds(half, half), at], sems.at[i]
+        )
+        copy.start()
+        copies.append(copy)
+    for copy in copies:
+        copy.wait()
+
+
+def finish(low, high, arrived):
+    half, columns = low.shape
+    return pl.pallas_call(
+        finish_kernel,
         out_shape=jax.ShapeDtypeStruct((2 * half, columns), jnp.bfloat16),
-        in_specs=[VMEM] * (3 + len(low) + len(high)),
-        out_specs=VMEM,
+        in_specs=[VMEM] * (2 + len(arrived)),
+        out_specs=HBM,
+        scratch_shapes=[
+            pltpu.VMEM((half, columns), jnp.bfloat16),
+            pltpu.SemaphoreType.DMA((5,)),
+        ],
         name="finish",
         compiler_params=PARAMS,
         cost_estimate=pl.CostEstimate(
-            flops=4 * half * mine.shape[1] * columns, bytes_accessed=12 << 20, transcendentals=0
-        ),
-    )(parts, mine, other, *low, *high)
+            flops=3 * half * columns, bytes_accessed=10 * half * columns, transcendentals=0
+        ),
+    )(low, high, *arrived)
 
 
 def exchange_body(queries, attn_keys, attn_values, out_proj):
@@ -352,8 +392,7 @@
         return swap(packed)
 
     def paired(own):
-        stacked = jnp.stack([array[1:] for array in own])
-        return own, pair_swap(stacked)
+        return own, [pair_swap(own[j]) for j in range(groups)]
 
     def attended(phase_inputs):
         outs = attention(phase_inputs, groups, half, width)
@@ -382,21 +421,19 @@
     parts_high = attended([low, high])
 
     share = swap([share] * groups)
-    mine = jnp.stack(share)
-    other = pair_swap(mine)
+    mine, other = paired(share)
 
     def line(parts):
         chunks = {}
         for tag in held:
-            chunks[tag] = project(parts, held[tag], f32)
+            chunks[tag] = project(parts, held[tag], bf16)
         last = [chunks["own"]]
         for t in range(tp_count - 1, 1, -1):
             arrived = None
             for l in range(t):
                 send = chunks[f"a{t}" if 2 * l < tp_count else f"b{t}"]
                 if arrived is not None:
-                    send = send + arrived.astype(f32)
-                send = send.astype(bf16)
+                    send = (send.astype(f32) + arrived.astype(f32)).astype(bf16)
                 pairs = [(l, l + 1), (tp_count - 1 - l, tp_count - 2 - l)]
                 arrived = lax.ppermute(send, "tp", pairs)
             last.append(arrived)
@@ -405,7 +442,8 @@
     low_sums = line(parts_low)
     high_sums = line(parts_high)
     near = lax.ppermute(jnp.stack(parts_low + parts_high), "tp", ends)
-    return finish(near, mine, other, low_sums, high_sums, groups)
+    low_rows, high_rows = near_sums(near, mine, other, low_sums, high_sums[0], groups)
+    return finish(low_rows, high_rows, high_sums[1:])
 
 
 def body(queries, attn_keys, attn_values, out_proj):

time: 186 us -> 158 us (0.85)
  waiting for transfers between devices: 119 us -> 93.2 us
  other arithmetic: 3.93 us -> 0.76 us
    ppermute x10, waiting for transfers between devices: 83.4 us -> 69.9 us  [line(): arrived = lax.ppermute(send, 'tp', pairs)]
    ppermute x15, waiting for transfers between devices: 35.8 us -> 23.2 us  [swap(): got[j] = lax.ppermute(arrays[j], 'ctx', pairs)]
    another operation x3 -> x0, other arithmetic: 3.04 us -> none  [the longest x2 1.74 us: paired(): stacked = jnp.stack([array[1:] for array in own])]
    ppermute x1, starting transfers between devices: 5.75 us -> 3.51 us  [exchange_body(): share = lax.ppermute(share, 'tp', ends)]
    ppermute x3 -> x12, starting transfers between devices: 0.01 us -> 2.12 us  [pair_swap(): return lax.ppermute(array, 'ctx', [(d, d ^ 1) for d in range(ctx_count)])]
  transfers between devices with their start and end apart: 30 -> 39, of which waited for: 14 -> 14; matrix products, arithmetic and copies ran while one was open for 2% -> 1% of each run, Pallas kernels for 12% -> 15%
where the time goes in v2:
time: 158 us; the launch traced here: 157 us
  waiting for transfers between devices  93.2 us (59%)
  starting transfers between devices  36.8 us (23%)
  Pallas kernels  25.8 us (16%)
    ppermute x10, waiting for transfers between devices, line(): arrived = lax.ppermute(send, 'tp', pairs)  69.9 us
    ppermute x15, waiting for transfers between devices, swap(): got[j] = lax.ppermute(arrays[j], 'ctx', pairs)  23.2 us
    ppermute x15, starting transfers between devices, swap(): got[j] = lax.ppermute(arrays[j], 'ctx', pairs)  19 us
    ppermute x10, starting transfers between devices, line(): arrived = lax.ppermute(send, 'tp', pairs)  10.8 us
    pallas_call x4, Pallas kernels, hold(): pl.pallas_call(hold_kernel, out_shape=jax.ShapeDtypeStruct((rows, columns...  9.15 us
    pallas_call x8, Pallas kernels, project(): pl.pallas_call(functools.partial(project_kernel, groups), out_shape=jax.S...  5.91 us
    pallas_call x2, Pallas kernels, attention(): pl.pallas_call(functools.partial(attention_kernel, groups, phases), out_s...  4.78 us
    ppermute x1, starting transfers between devices, exchange_body(): share = lax.ppermute(share, 'tp', ends)  3.51 us
  transfers between devices with their start and end apart: 39, of which 14 were waited for; matrix products, arithmetic and copies ran while one was open for 1% of the time, Pallas kernels for 15%

profile of v2, /device:TPU:0, one launch (start us, length us, event | category | flops | bytes accessed | tf_op | source)
XLA Modules:
  0.0 157.2 jit_solution(7772983313399854068)
XLA Ops:
  0.0 1.3 shard_map.48
  1.3 3.0 %collective-permute-start.10 = (bf16[3,128,256]{2,1,0:T(8,128)(2,1)S(1)}, bf16[3,128,256]{2,1,0:T(8,128)(2,1)S(1)}, u32[]{:S(2)}, u32[]{:S(2)}) collective-permute-start(bf16[3,128,256]{2,1,0:T(8,128)(2,1)S(1)} %get-tuple-element.32), channel_id=1, source_target_pairs={{0,8},{4,12},{8,0},{12,4},{16,24},{20,28},{24,16},{28,20},{1,9},{5... | collective-permute-start | bytes 589832 | tf_op jit(solution)/shard_map/ppermute | solution.py:384
  4.3 1.5 collective-permute-start.11
  5.9 1.3 shard_map.46
  7.1 2.0 %collective-permute-start = (bf16[3,128,256]{2,1,0:T(8,128)(2,1)S(1)}, bf16[3,128,256]{2,1,0:T(8,128)(2,1)S(1)}, u32[]{:S(2)}, u32[]{:S(2)}) collective-permute-start(bf16[3,128,256]{2,1,0:T(8,128)(2,1)S(1)} %get-tuple-element.24), channel_id=1, source_target_pairs={{0,8},{4,12},{8,0},{12,4},{16,24},{20,28},{24,16},{28,20},{1,9},{5... | collective-permute-start | bytes 589832 | tf_op jit(solution)/shard_map/ppermute | solution.py:384
  9.1 0.9 collective-permute-done.10.refs_9_
  10.1 2.0 %collective-permute-start.1 = (bf16[3,128,256]{2,1,0:T(8,128)(2,1)S(1)}, bf16[3,128,256]{2,1,0:T(8,128)(2,1)S(1)}, u32[]{:S(2)}, u32[]{:S(2)}) collective-permute-start(bf16[3,128,256]{2,1,0:T(8,128)(2,1)S(1)} %get-tuple-element.25), channel_id=1, source_target_pairs={{0,16},{4,20},{8,24},{12,28},{16,0},{20,4},{24,8},{28,12},{1,17},{... | collective-permute-start | bytes 589832 | tf_op jit(solution)/shard_map/ppermute | solution.py:384
  12.1 3.2 %collective-permute-done.11.refs_10_ = bf16[3,128,256]{2,1,0:T(8,128)(2,1)S(1)} collective-permute-done((bf16[3,128,256]{2,1,0:T(8,128)(2,1)S(1)}, bf16[3,128,256]{2,1,0:T(8,128)(2,1)S(1)}, u32[]{:S(2)}, u32[]{:S(2)}) %collective-permute-start.11) | collective-permute-done | bytes 196640 | tf_op jit(solution)/shard_map/ppermute | solution.py:384
  15.3 0.6 collective-permute-start.2
  15.9 0.5 collective-permute-start.14
  16.4 2.1 %collective-permute-done.refs_1_ = bf16[3,128,256]{2,1,0:T(8,128)(2,1)S(1)} collective-permute-done((bf16[3,128,256]{2,1,0:T(8,128)(2,1)S(1)}, bf16[3,128,256]{2,1,0:T(8,128)(2,1)S(1)}, u32[]{:S(2)}, u32[]{:S(2)}) %collective-permute-start) | collective-permute-done | bytes 196640 | tf_op jit(solution)/shard_map/ppermute | solution.py:384
  18.5 4.8 %collective-permute-done.1.refs_2_ = bf16[3,128,256]{2,1,0:T(8,128)(2,1)S(1)} collective-permute-done((bf16[3,128,256]{2,1,0:T(8,128)(2,1)S(1)}, bf16[3,128,256]{2,1,0:T(8,128)(2,1)S(1)}, u32[]{:S(2)}, u32[]{:S(2)}) %collective-permute-start.1) | collective-permute-done | bytes 196640 | tf_op jit(solution)/shard_map/ppermute | solution.py:384
  23.3 0.5 collective-permute-start.4
  23.9 0.4 collective-permute-start.6
  24.3 1.0 piece.1
  25.4 2.3 %shard_map.53.refs_4_ = bf16[1024,2048]{1,0:T(8,128)(2,1)S(1)} custom-call(s32[1]{0:T(128)} %bitcast.9.place_ref, bf16[1024,8192]{1,0:T(8,128)(2,1)} %w_ref.9), custom_call_target="tpu_custom_call" | custom-call | bytes 8388608 | tf_op jit(solution)/shard_map/pallas_call | solution.py:234
  27.7 2.3 %shard_map.57.refs_4_ = bf16[1024,2048]{1,0:T(8,128)(2,1)S(1)} custom-call(s32[1]{0:T(128)} %bitcast.11.place_ref, bf16[1024,8192]{1,0:T(8,128)(2,1)} %w_ref.9), custom_call_target="tpu_custom_call" | custom-call | bytes 8388608 | tf_op jit(solution)/shard_map/pallas_call | solution.py:234
  30.0 2.3 %shard_map.55.refs_4_ = bf16[1024,2048]{1,0:T(8,128)(2,1)S(1)} custom-call(s32[1]{0:T(128)} %bitcast.10.place_ref, bf16[1024,8192]{1,0:T(8,128)(2,1)} %w_ref.9), custom_call_target="tpu_custom_call" | custom-call | bytes 8388608 | tf_op jit(solution)/shard_map/pallas_call | solution.py:234
  32.3 3.5 %collective-permute-start.21 = (bf16[1024,256]{1,0:T(8,128)(2,1)S(1)}, bf16[1024,256]{1,0:T(8,128)(2,1)S(1)}, u32[]{:S(2)}, u32[]{:S(2)}) collective-permute-start(bf16[1024,256]{1,0:T(8,128)(2,1)S(1)} %piece.1), channel_id=1, source_target_pairs={{0,1},{3,2},{4,5},{7,6},{8,9},{11,10},{12,13},{15,14},{16,17},{19,... | collective-permute-start | bytes 1572872 | tf_op jit(solution)/shard_map/ppermute | solution.py:407
  35.9 3.4 %shard_map.49 = (bf16[128,256]{1,0:T(8,128)(2,1)S(1)}, bf16[128,256]{1,0:T(8,128)(2,1)S(1)}, bf16[128,256]{1,0:T(8,128)(2,1)S(1)}, bf16[128,256]{1,0:T(8,128)(2,1)S(1)}) custom-call(bf16[3,128,256]{2,1,0:T(8,128)(2,1)S(1)} %get-tuple-element.23.refs_0_, bf16[3,128,256]{2,1,0:T(8,128)(2,1)S(1)} %collective-permute-done.refs_1_, ...), custom_call_target="tpu_custom_call" | custom-call | flops 872415232 | bytes 2097152 | tf_op jit(solution)/shard_map/pallas_call | solution.py:209
  39.3 0.9 collective-permute-start.17
  40.2 1.3 shard_map.47
  41.6 1.2 collective-permute-start.7
  42.8 1.5 collective-permute-start.8
  44.3 0.8 collective-permute-start.9
  45.1 0.8 collective-permute-done.7.refs_1_
  46.0 1.1 collective-permute-start.18
  47.1 0.9 collective-permute-done.8.refs_2_
  48.0 1.6 collective-permute-start.19
  49.5 0.5 collective-permute-done.9.refs_3_
  50.1 0.7 shard_map.58
  50.8 1.3 collective-permute-start.32
  52.3 0.9 collective-permute-done.19.refs_3_
  53.2 1.3 collective-permute-start.20
  54.5 0.7 shard_map.61
  55.2 1.3 collective-permute-start.37
  56.5 0.7 shard_map.56
  57.3 1.5 collective-permute-start.29
  58.8 0.7 shard_map.59
  59.6 0.8 shard_map.54
  60.3 0.7 shard_map.60
  61.1 1.3 collective-permute-start.34
  62.4 2.0 %collective-permute-done.32 = bf16[128,2048]{1,0:T(8,128)(2,1)S(1)} collective-permute-done((bf16[128,2048]{1,0:T(8,128)(2,1)S(1)}, bf16[128,2048]{1,0:T(8,128)(2,1)S(1)}, u32[]{:S(2)}, u32[]{:S(2)}) %collective-permute-start.32) | collective-permute-done | bytes 524320 | tf_op jit(solution)/shard_map/ppermute | solution.py:438
  64.6 33.6 %collective-permute-done.29 = bf16[128,2048]{1,0:T(8,128)(2,1)S(1)} collective-permute-done((bf16[128,2048]{1,0:T(8,128)(2,1)S(1)}, bf16[128,2048]{1,0:T(8,128)(2,1)S(1)}, u32[]{:S(2)}, u32[]{:S(2)}) %collective-permute-start.29) | collective-permute-done | bytes 524320 | tf_op jit(solution)/shard_map/ppermute | solution.py:438
  98.1 0.8 collective-permute-start.24
  99.1 6.9 %collective-permute-done.34 = bf16[128,2048]{1,0:T(8,128)(2,1)S(1)} collective-permute-done((bf16[128,2048]{1,0:T(8,128)(2,1)S(1)}, bf16[128,2048]{1,0:T(8,128)(2,1)S(1)}, u32[]{:S(2)}, u32[]{:S(2)}) %collective-permute-start.34) | collective-permute-done | bytes 524320 | tf_op jit(solution)/shard_map/ppermute | solution.py:438
  106.0 0.7 collective-permute-start.30
  106.8 0.8 collective-permute-start.23
  107.6 1.0 collective-permute-start.22
  108.7 0.7 collective-permute-start.35
  109.3 0.1 add_convert_fusion
  109.5 0.7 collective-permute-start.33
  110.4 9.0 %collective-permute-done.23.refs_3_ = bf16[1024,256]{1,0:T(8,128)(2,1)S(1)} collective-permute-done((bf16[1024,256]{1,0:T(8,128)(2,1)S(1)}, bf16[1024,256]{1,0:T(8,128)(2,1)S(1)}, u32[]{:S(2)}, u32[]{:S(2)}) %collective-permute-start.23) | collective-permute-done | bytes 524320 | tf_op jit(solution)/shard_map/ppermute | solution.py:384
  119.4 0.5 collective-permute-start.26
  120.0 1.3 collective-permute-start.31
  121.4 0.7 collective-permute-start.38
  122.1 1.3 collective-permute-start.36
  123.4 2.3 %shard_map.50.refs_4_ = bf16[1024,2048]{1,0:T(8,128)(2,1)S(1)} custom-call(s32[1]{0:T(128)} %bitcast.8.place_ref, bf16[1024,8192]{1,0:T(8,128)(2,1)} %w_ref.9), custom_call_target="tpu_custom_call" | custom-call | bytes 8388608 | tf_op jit(solution)/shard_map/pallas_call | solution.py:234
  125.7 0.7 shard_map.52.refs_10_
  126.4 0.7 shard_map.51.refs_9_
  127.2 17.8 %collective-permute-done.31.refs_11_ = bf16[128,2048]{1,0:T(8,128)(2,1)S(1)} collective-permute-done((bf16[128,2048]{1,0:T(8,128)(2,1)S(1)}, bf16[128,2048]{1,0:T(8,128)(2,1)S(1)}, u32[]{:S(2)}, u32[]{:S(2)}) %collective-permute-start.31) | collective-permute-done | bytes 524320 | tf_op jit(solution)/shard_map/ppermute | solution.py:438
  145.0 1.3 nsum.1
  146.3 9.7 %collective-permute-done.36.refs_0_ = bf16[128,2048]{1,0:T(8,128)(2,1)S(1)} collective-permute-done((bf16[128,2048]{1,0:T(8,128)(2,1)S(1)}, bf16[128,2048]{1,0:T(8,128)(2,1)S(1)}, u32[]{:S(2)}, u32[]{:S(2)}) %collective-permute-start.36) | collective-permute-done | bytes 524320 | tf_op jit(solution)/shard_map/ppermute | solution.py:438
  156.0 1.0 finish.1
  (47 shorter events, 0.9 us)
Async XLA Ops:
  1.3 8.8 %collective-permute-start.10 = (bf16[3,128,256]{2,1,0:T(8,128)(2,1)S(1)}, bf16[3,128,256]{2,1,0:T(8,128)(2,1)S(1)}, u32[]{:S(2)}, u32[]{:S(2)}) collective-permute-start(bf16[3,128,256]{2,1,0:T(8,128)(2,1)S(1)} %get-tuple-element.32), channel_id=1, source_target_pairs={{0,8},{4,12},{8,0},{12,4},{16,24},{20,28},{24,16},{28,20},{1,9},{5... | collective-permute-start | bytes 589832 | tf_op jit(solution)/shard_map/ppermute | solution.py:384
  4.3 11.0 %collective-permute-start.11 = (bf16[3,128,256]{2,1,0:T(8,128)(2,1)S(1)}, bf16[3,128,256]{2,1,0:T(8,128)(2,1)S(1)}, u32[]{:S(2)}, u32[]{:S(2)}) collective-permute-start(bf16[3,128,256]{2,1,0:T(8,128)(2,1)S(1)} %get-tuple-element.33), channel_id=1, source_target_pairs={{0,16},{4,20},{8,24},{12,28},{16,0},{20,4},{24,8},{28,12},{1,17},{... | collective-permute-start | bytes 589832 | tf_op jit(solution)/shard_map/ppermute | solution.py:384
  5.8 10.1 %collective-permute-start.12 = (bf16[3,128,256]{2,1,0:T(8,128)(2,1)S(1)}, bf16[3,128,256]{2,1,0:T(8,128)(2,1)S(1)}, u32[]{:S(2)}, u32[]{:S(2)}) collective-permute-start(bf16[3,128,256]{2,1,0:T(8,128)(2,1)S(1)} %get-tuple-element.34), channel_id=1, source_target_pairs={{0,24},{4,28},{8,16},{12,20},{16,8},{20,12},{24,0},{28,4},{1,25},{... | collective-permute-start | bytes 589832 | tf_op jit(solution)/shard_map/ppermute | solution.py:384
  5.8 10.1 %collective-permute-start.13 = (bf16[3,128,256]{2,1,0:T(8,128)(2,1)S(1)}, bf16[3,128,256]{2,1,0:T(8,128)(2,1)S(1)}, u32[]{:S(2)}, u32[]{:S(2)}) collective-permute-start(bf16[3,128,256]{2,1,0:T(8,128)(2,1)S(1)} %get-tuple-element.31.refs_8_), channel_id=1, source_target_pairs={{0,4},{4,0},{8,12},{12,8},{16,20},{20,16},{24,28},{28,24},{1,5},{5... | collective-permute-start | bytes 589832 | tf_op jit(solution)/shard_map/ppermute | solution.py:388
  7.1 11.4 %collective-permute-start = (bf16[3,128,256]{2,1,0:T(8,128)(2,1)S(1)}, bf16[3,128,256]{2,1,0:T(8,128)(2,1)S(1)}, u32[]{:S(2)}, u32[]{:S(2)}) collective-permute-start(bf16[3,128,256]{2,1,0:T(8,128)(2,1)S(1)} %get-tuple-element.24), channel_id=1, source_target_pairs={{0,8},{4,12},{8,0},{12,4},{16,24},{20,28},{24,16},{28,20},{1,9},{5... | collective-permute-start | bytes 589832 | tf_op jit(solution)/shard_map/ppermute | solution.py:384
  10.1 13.2 %collective-permute-start.1 = (bf16[3,128,256]{2,1,0:T(8,128)(2,1)S(1)}, bf16[3,128,256]{2,1,0:T(8,128)(2,1)S(1)}, u32[]{:S(2)}, u32[]{:S(2)}) collective-permute-start(bf16[3,128,256]{2,1,0:T(8,128)(2,1)S(1)} %get-tuple-element.25), channel_id=1, source_target_pairs={{0,16},{4,20},{8,24},{12,28},{16,0},{20,4},{24,8},{28,12},{1,17},{... | collective-permute-start | bytes 589832 | tf_op jit(solution)/shard_map/ppermute | solution.py:384
  15.3 8.0 %collective-permute-start.2 = (bf16[3,128,256]{2,1,0:T(8,128)(2,1)S(1)}, bf16[3,128,256]{2,1,0:T(8,128)(2,1)S(1)}, u32[]{:S(2)}, u32[]{:S(2)}) collective-permute-start(bf16[3,128,256]{2,1,0:T(8,128)(2,1)S(1)} %get-tuple-element.26), channel_id=1, source_target_pairs={{0,24},{4,28},{8,16},{12,20},{16,8},{20,12},{24,0},{28,4},{1,25},{... | collective-permute-start | bytes 589832 | tf_op jit(solution)/shard_map/ppermute | solution.py:384
  15.9 7.9 %collective-permute-start.3 = (bf16[3,128,256]{2,1,0:T(8,128)(2,1)S(1)}, bf16[3,128,256]{2,1,0:T(8,128)(2,1)S(1)}, u32[]{:S(2)}, u32[]{:S(2)}) collective-permute-start(bf16[3,128,256]{2,1,0:T(8,128)(2,1)S(1)} %get-tuple-element.23.refs_0_), channel_id=1, source_target_pairs={{0,4},{4,0},{8,12},{12,8},{16,20},{20,16},{24,28},{28,24},{1,5},{5... | collective-permute-start | bytes 589832 | tf_op jit(solution)/shard_map/ppermute | solution.py:388
  15.9 8.0 %collective-permute-start.14 = (bf16[3,128,256]{2,1,0:T(8,128)(2,1)S(1)}, bf16[3,128,256]{2,1,0:T(8,128)(2,1)S(1)}, u32[]{:S(2)}, u32[]{:S(2)}) collective-permute-start(bf16[3,128,256]{2,1,0:T(8,128)(2,1)S(1)} %collective-permute-done.10.refs_9_), channel_id=1, source_target_pairs={{0,4},{4,0},{8,12},{12,8},{16,20},{20,16},{24,28},{28,24},{1,5},{5... | collective-permute-start | bytes 589832 | tf_op jit(solution)/shard_map/ppermute | solution.py:388
  18.5 13.8 %collective-permute-start.15 = (bf16[3,128,256]{2,1,0:T(8,128)(2,1)S(1)}, bf16[3,128,256]{2,1,0:T(8,128)(2,1)S(1)}, u32[]{:S(2)}, u32[]{:S(2)}) collective-permute-start(bf16[3,128,256]{2,1,0:T(8,128)(2,1)S(1)} %collective-permute-done.11.refs_10_), channel_id=1, source_target_pairs={{0,4},{4,0},{8,12},{12,8},{16,20},{20,16},{24,28},{28,24},{1,5},{5... | collective-permute-start | bytes 589832 | tf_op jit(solution)/shard_map/ppermute | solution.py:388
  23.3 12.5 %collective-permute-start.16 = (bf16[3,128,256]{2,1,0:T(8,128)(2,1)S(1)}, bf16[3,128,256]{2,1,0:T(8,128)(2,1)S(1)}, u32[]{:S(2)}, u32[]{:S(2)}) collective-permute-start(bf16[3,128,256]{2,1,0:T(8,128)(2,1)S(1)} %collective-permute-done.12.refs_11_), channel_id=1, source_target_pairs={{0,4},{4,0},{8,12},{12,8},{16,20},{20,16},{24,28},{28,24},{1,5},{5... | collective-permute-start | bytes 589832 | tf_op jit(solution)/shard_map/ppermute | solution.py:388
  23.3 12.5 %collective-permute-start.4 = (bf16[3,128,256]{2,1,0:T(8,128)(2,1)S(1)}, bf16[3,128,256]{2,1,0:T(8,128)(2,1)S(1)}, u32[]{:S(2)}, u32[]{:S(2)}) collective-permute-start(bf16[3,128,256]{2,1,0:T(8,128)(2,1)S(1)} %collective-permute-done.refs_1_), channel_id=1, source_target_pairs={{0,4},{4,0},{8,12},{12,8},{16,20},{20,16},{24,28},{28,24},{1,5},{5... | collective-permute-start | bytes 589832 | tf_op jit(solution)/shard_map/ppermute | solution.py:388
  23.8 12.0 %collective-permute-start.5 = (bf16[3,128,256]{2,1,0:T(8,128)(2,1)S(1)}, bf16[3,128,256]{2,1,0:T(8,128)(2,1)S(1)}, u32[]{:S(2)}, u32[]{:S(2)}) collective-permute-start(bf16[3,128,256]{2,1,0:T(8,128)(2,1)S(1)} %collective-permute-done.1.refs_2_), channel_id=1, source_target_pairs={{0,4},{4,0},{8,12},{12,8},{16,20},{20,16},{24,28},{28,24},{1,5},{5... | collective-permute-start | bytes 589832 | tf_op jit(solution)/shard_map/ppermute | solution.py:388
  23.9 12.0 %collective-permute-start.6 = (bf16[3,128,256]{2,1,0:T(8,128)(2,1)S(1)}, bf16[3,128,256]{2,1,0:T(8,128)(2,1)S(1)}, u32[]{:S(2)}, u32[]{:S(2)}) collective-permute-start(bf16[3,128,256]{2,1,0:T(8,128)(2,1)S(1)} %collective-permute-done.2.refs_3_), channel_id=1, source_target_pairs={{0,4},{4,0},{8,12},{12,8},{16,20},{20,16},{24,28},{28,24},{1,5},{5... | collective-permute-start | bytes 589832 | tf_op jit(solution)/shard_map/ppermute | solution.py:388
  32.3 28.8 %collective-permute-start.21 = (bf16[1024,256]{1,0:T(8,128)(2,1)S(1)}, bf16[1024,256]{1,0:T(8,128)(2,1)S(1)}, u32[]{:S(2)}, u32[]{:S(2)}) collective-permute-start(bf16[1024,256]{1,0:T(8,128)(2,1)S(1)} %piece.1), channel_id=1, source_target_pairs={{0,1},{3,2},{4,5},{7,6},{8,9},{11,10},{12,13},{15,14},{16,17},{19,... | collective-permute-start | bytes 1572872 | tf_op jit(solution)/shard_map/ppermute | solution.py:407
  39.3 12.9 %collective-permute-start.17 = (bf16[128,256]{1,0:T(8,128)(2,1)S(1)}, bf16[128,256]{1,0:T(8,128)(2,1)S(1)}, u32[]{:S(2)}, u32[]{:S(2)}) collective-permute-start(bf16[128,256]{1,0:T(8,128)(2,1)S(1)} %get-tuple-element.36), channel_id=1, source_target_pairs={{0,8},{4,12},{8,0},{12,4},{16,24},{20,28},{24,16},{28,20},{1,9},{5... | collective-permute-start | bytes 196616 | tf_op jit(solution)/shard_map/ppermute | solution.py:384
  41.6 4.4 %collective-permute-start.7 = (bf16[128,256]{1,0:T(8,128)(2,1)S(1)}, bf16[128,256]{1,0:T(8,128)(2,1)S(1)}, u32[]{:S(2)}, u32[]{:S(2)}) collective-permute-start(bf16[128,256]{1,0:T(8,128)(2,1)S(1)} %get-tuple-element.28), channel_id=1, source_target_pairs={{0,8},{4,12},{8,0},{12,4},{16,24},{20,28},{24,16},{28,20},{1,9},{5... | collective-permute-start | bytes 196616 | tf_op jit(solution)/shard_map/ppermute | solution.py:384
  42.8 5.2 %collective-permute-start.8 = (bf16[128,256]{1,0:T(8,128)(2,1)S(1)}, bf16[128,256]{1,0:T(8,128)(2,1)S(1)}, u32[]{:S(2)}, u32[]{:S(2)}) collective-permute-start(bf16[128,256]{1,0:T(8,128)(2,1)S(1)} %get-tuple-element.29), channel_id=1, source_target_pairs={{0,16},{4,20},{8,24},{12,28},{16,0},{20,4},{24,8},{28,12},{1,17},{... | collective-permute-start | bytes 196616 | tf_op jit(solution)/shard_map/ppermute | solution.py:384
  44.3 5.8 %collective-permute-start.9 = (bf16[128,256]{1,0:T(8,128)(2,1)S(1)}, bf16[128,256]{1,0:T(8,128)(2,1)S(1)}, u32[]{:S(2)}, u32[]{:S(2)}) collective-permute-start(bf16[128,256]{1,0:T(8,128)(2,1)S(1)} %get-tuple-element.30), channel_id=1, source_target_pairs={{0,24},{4,28},{8,16},{12,20},{16,8},{20,12},{24,0},{28,4},{1,25},{... | collective-permute-start | bytes 196616 | tf_op jit(solution)/shard_map/ppermute | solution.py:384
  46.0 6.3 %collective-permute-start.18 = (bf16[128,256]{1,0:T(8,128)(2,1)S(1)}, bf16[128,256]{1,0:T(8,128)(2,1)S(1)}, u32[]{:S(2)}, u32[]{:S(2)}) collective-permute-start(bf16[128,256]{1,0:T(8,128)(2,1)S(1)} %get-tuple-element.37), channel_id=1, source_target_pairs={{0,16},{4,20},{8,24},{12,28},{16,0},{20,4},{24,8},{28,12},{1,17},{... | collective-permute-start | bytes 196616 | tf_op jit(solution)/shard_map/ppermute | solution.py:384
  48.0 5.2 %collective-permute-start.19 = (bf16[128,256]{1,0:T(8,128)(2,1)S(1)}, bf16[128,256]{1,0:T(8,128)(2,1)S(1)}, u32[]{:S(2)}, u32[]{:S(2)}) collective-permute-start(bf16[128,256]{1,0:T(8,128)(2,1)S(1)} %get-tuple-element.38), channel_id=1, source_target_pairs={{0,24},{4,28},{8,16},{12,20},{16,8},{20,12},{24,0},{28,4},{1,25},{... | collective-permute-start | bytes 196616 | tf_op jit(solution)/shard_map/ppermute | solution.py:384
  50.8 13.6 %collective-permute-start.32 = (bf16[128,2048]{1,0:T(8,128)(2,1)S(1)}, bf16[128,2048]{1,0:T(8,128)(2,1)S(1)}, u32[]{:S(2)}, u32[]{:S(2)}) collective-permute-start(bf16[128,2048]{1,0:T(8,128)(2,1)S(1)} %shard_map.58), channel_id=1, source_target_pairs={{0,1},{3,2},{4,5},{7,6},{8,9},{11,10},{12,13},{15,14},{16,17},{19,... | collective-permute-start | bytes 1572872 | tf_op jit(solution)/shard_map/ppermute | solution.py:438
  53.2 53.7 %collective-permute-start.20 = (bf16[8,128,256]{2,1,0:T(8,128)(2,1)S(1)}, bf16[8,128,256]{2,1,0:T(8,128)(2,1)S(1)}, u32[]{:S(2)}, u32[]{:S(2)}) collective-permute-start(bf16[8,128,256]{2,1,0:T(8,128)(2,1)S(1)} %bitcast_dynamic-update-slice_fusion), channel_id=1, source_target_pairs={{0,1},{3,2},{4,5},{7,6},{8,9},{11,10},{12,13},{15,14},{16,17},{19,... | collective-permute-start | bytes 1572872 | tf_op jit(solution)/shard_map/ppermute | solution.py:444
  55.2 52.4 %collective-permute-start.37 = (bf16[128,2048]{1,0:T(8,128)(2,1)S(1)}, bf16[128,2048]{1,0:T(8,128)(2,1)S(1)}, u32[]{:S(2)}, u32[]{:S(2)}) collective-permute-start(bf16[128,2048]{1,0:T(8,128)(2,1)S(1)} %shard_map.61), channel_id=1, source_target_pairs={{0,1},{3,2},{4,5},{7,6},{8,9},{11,10},{12,13},{15,14},{16,17},{19,... | collective-permute-start | bytes 1572872 | tf_op jit(solution)/shard_map/ppermute | solution.py:438
  57.3 40.8 %collective-permute-start.29 = (bf16[128,2048]{1,0:T(8,128)(2,1)S(1)}, bf16[128,2048]{1,0:T(8,128)(2,1)S(1)}, u32[]{:S(2)}, u32[]{:S(2)}) collective-permute-start(bf16[128,2048]{1,0:T(8,128)(2,1)S(1)} %shard_map.56), channel_id=1, source_target_pairs={{0,1},{3,2},{4,5},{7,6},{8,9},{11,10},{12,13},{15,14},{16,17},{19,... | collective-permute-start | bytes 1572872 | tf_op jit(solution)/shard_map/ppermute | solution.py:438
  61.1 44.9 %collective-permute-start.34 = (bf16[128,2048]{1,0:T(8,128)(2,1)S(1)}, bf16[128,2048]{1,0:T(8,128)(2,1)S(1)}, u32[]{:S(2)}, u32[]{:S(2)}) collective-permute-start(bf16[128,2048]{1,0:T(8,128)(2,1)S(1)} %shard_map.60), channel_id=1, source_target_pairs={{0,1},{3,2},{4,5},{7,6},{8,9},{11,10},{12,13},{15,14},{16,17},{19,... | collective-permute-start | bytes 1572872 | tf_op jit(solution)/shard_map/ppermute | solution.py:438
  64.4 44.2 %collective-permute-start.25 = (bf16[1024,256]{1,0:T(8,128)(2,1)S(1)}, bf16[1024,256]{1,0:T(8,128)(2,1)S(1)}, u32[]{:S(2)}, u32[]{:S(2)}) collective-permute-start(bf16[1024,256]{1,0:T(8,128)(2,1)S(1)} %collective-permute-done.21.refs_1_), channel_id=1, source_target_pairs={{0,4},{4,0},{8,12},{12,8},{16,20},{20,16},{24,28},{28,24},{1,5},{5... | collective-permute-start | bytes 1572872 | tf_op jit(solution)/shard_map/ppermute | solution.py:388
  98.1 11.4 %collective-permute-start.24 = (bf16[1024,256]{1,0:T(8,128)(2,1)S(1)}, bf16[1024,256]{1,0:T(8,128)(2,1)S(1)}, u32[]{:S(2)}, u32[]{:S(2)}) collective-permute-start(bf16[1024,256]{1,0:T(8,128)(2,1)S(1)} %collective-permute-done.21.refs_1_), channel_id=1, source_target_pairs={{0,24},{4,28},{8,16},{12,20},{16,8},{20,12},{24,0},{28,4},{1,25},{... | collective-permute-start | bytes 1572872 | tf_op jit(solution)/shard_map/ppermute | solution.py:384
  106.0 4.2 %collective-permute-start.30 = (bf16[128,2048]{1,0:T(8,128)(2,1)S(1)}, bf16[128,2048]{1,0:T(8,128)(2,1)S(1)}, u32[]{:S(2)}, u32[]{:S(2)}) collective-permute-start(bf16[128,2048]{1,0:T(8,128)(2,1)S(1)} %add_convert_fusion.5), channel_id=1, source_target_pairs={{1,2},{2,1},{5,6},{6,5},{9,10},{10,9},{13,14},{14,13},{17,18},{18,... | collective-permute-start | bytes 1572872 | tf_op jit(solution)/shard_map/ppermute | solution.py:438
  106.8 12.6 %collective-permute-start.23 = (bf16[1024,256]{1,0:T(8,128)(2,1)S(1)}, bf16[1024,256]{1,0:T(8,128)(2,1)S(1)}, u32[]{:S(2)}, u32[]{:S(2)}) collective-permute-start(bf16[1024,256]{1,0:T(8,128)(2,1)S(1)} %collective-permute-done.21.refs_1_), channel_id=1, source_target_pairs={{0,16},{4,20},{8,24},{12,28},{16,0},{20,4},{24,8},{28,12},{1,17},{... | collective-permute-start | bytes 1572872 | tf_op jit(solution)/shard_map/ppermute | solution.py:384
  107.6 11.8 %collective-permute-start.22 = (bf16[1024,256]{1,0:T(8,128)(2,1)S(1)}, bf16[1024,256]{1,0:T(8,128)(2,1)S(1)}, u32[]{:S(2)}, u32[]{:S(2)}) collective-permute-start(bf16[1024,256]{1,0:T(8,128)(2,1)S(1)} %collective-permute-done.21.refs_1_), channel_id=1, source_target_pairs={{0,8},{4,12},{8,0},{12,4},{16,24},{20,28},{24,16},{28,20},{1,9},{5... | collective-permute-start | bytes 1572872 | tf_op jit(solution)/shard_map/ppermute | solution.py:384
  108.7 11.3 %collective-permute-start.35 = (bf16[128,2048]{1,0:T(8,128)(2,1)S(1)}, bf16[128,2048]{1,0:T(8,128)(2,1)S(1)}, u32[]{:S(2)}, u32[]{:S(2)}) collective-permute-start(bf16[128,2048]{1,0:T(8,128)(2,1)S(1)} %add_convert_fusion.2), channel_id=1, source_target_pairs={{1,2},{2,1},{5,6},{6,5},{9,10},{10,9},{13,14},{14,13},{17,18},{18,... | collective-permute-start | bytes 1572872 | tf_op jit(solution)/shard_map/ppermute | solution.py:438
  109.5 11.9 %collective-permute-start.33 = (bf16[128,2048]{1,0:T(8,128)(2,1)S(1)}, bf16[128,2048]{1,0:T(8,128)(2,1)S(1)}, u32[]{:S(2)}, u32[]{:S(2)}) collective-permute-start(bf16[128,2048]{1,0:T(8,128)(2,1)S(1)} %add_convert_fusion.3), channel_id=1, source_target_pairs={{1,2},{2,1},{5,6},{6,5},{9,10},{10,9},{13,14},{14,13},{17,18},{18,... | collective-permute-start | bytes 1572872 | tf_op jit(solution)/shard_map/ppermute | solution.py:438
  110.2 11.9 %collective-permute-start.28 = (bf16[1024,256]{1,0:T(8,128)(2,1)S(1)}, bf16[1024,256]{1,0:T(8,128)(2,1)S(1)}, u32[]{:S(2)}, u32[]{:S(2)}) collective-permute-start(bf16[1024,256]{1,0:T(8,128)(2,1)S(1)} %collective-permute-done.24.refs_4_), channel_id=1, source_target_pairs={{0,4},{4,0},{8,12},{12,8},{16,20},{20,16},{24,28},{28,24},{1,5},{5... | collective-permute-start | bytes 1572872 | tf_op jit(solution)/shard_map/ppermute | solution.py:388
  119.4 7.8 %collective-permute-start.27 = (bf16[1024,256]{1,0:T(8,128)(2,1)S(1)}, bf16[1024,256]{1,0:T(8,128)(2,1)S(1)}, u32[]{:S(2)}, u32[]{:S(2)}) collective-permute-start(bf16[1024,256]{1,0:T(8,128)(2,1)S(1)} %collective-permute-done.23.refs_3_), channel_id=1, source_target_pairs={{0,4},{4,0},{8,12},{12,8},{16,20},{20,16},{24,28},{28,24},{1,5},{5... | collective-permute-start | bytes 1572872 | tf_op jit(solution)/shard_map/ppermute | solution.py:388
  119.4 7.8 %collective-permute-start.26 = (bf16[1024,256]{1,0:T(8,128)(2,1)S(1)}, bf16[1024,256]{1,0:T(8,128)(2,1)S(1)}, u32[]{:S(2)}, u32[]{:S(2)}) collective-permute-start(bf16[1024,256]{1,0:T(8,128)(2,1)S(1)} %collective-permute-done.22.refs_2_), channel_id=1, source_target_pairs={{0,4},{4,0},{8,12},{12,8},{16,20},{20,16},{24,28},{28,24},{1,5},{5... | collective-permute-start | bytes 1572872 | tf_op jit(solution)/shard_map/ppermute | solution.py:388
  120.0 25.0 %collective-permute-start.31 = (bf16[128,2048]{1,0:T(8,128)(2,1)S(1)}, bf16[128,2048]{1,0:T(8,128)(2,1)S(1)}, u32[]{:S(2)}, u32[]{:S(2)}) collective-permute-start(bf16[128,2048]{1,0:T(8,128)(2,1)S(1)} %add_convert_fusion.4), channel_id=1, source_target_pairs={{2,3},{1,0},{6,7},{5,4},{10,11},{9,8},{14,15},{13,12},{18,19},{17,... | collective-permute-start | bytes 1572872 | tf_op jit(solution)/shard_map/ppermute | solution.py:438
  121.4 24.9 %collective-permute-start.38 = (bf16[128,2048]{1,0:T(8,128)(2,1)S(1)}, bf16[128,2048]{1,0:T(8,128)(2,1)S(1)}, u32[]{:S(2)}, u32[]{:S(2)}) collective-permute-start(bf16[128,2048]{1,0:T(8,128)(2,1)S(1)} %add_convert_fusion), channel_id=1, source_target_pairs={{1,2},{2,1},{5,6},{6,5},{9,10},{10,9},{13,14},{14,13},{17,18},{18,... | collective-permute-start | bytes 1572872 | tf_op jit(solution)/shard_map/ppermute | solution.py:438
  122.1 33.9 %collective-permute-start.36 = (bf16[128,2048]{1,0:T(8,128)(2,1)S(1)}, bf16[128,2048]{1,0:T(8,128)(2,1)S(1)}, u32[]{:S(2)}, u32[]{:S(2)}) collective-permute-start(bf16[128,2048]{1,0:T(8,128)(2,1)S(1)} %add_convert_fusion.1), channel_id=1, source_target_pairs={{2,3},{1,0},{6,7},{5,4},{10,11},{9,8},{14,15},{13,12},{18,19},{17,... | collective-permute-start | bytes 1572872 | tf_op jit(solution)/shard_map/ppermute | solution.py:438

commit v3 on v2

--- a/solution.py
+++ b/solution.py
@@ -285,7 +285,8 @@
 
 def near_kernel(groups, *refs):
     parts_ref, mine, other = refs[0], refs[1 : groups + 1], refs[groups + 1 : 2 * groups + 1]
-    sums, outs = refs[2 * groups + 1 : -2], refs[-2:]
+    sums, out_ref, high_ref, low_s, sem = refs[2 * groups + 1 : -4], *refs[-4:]
+    outs = (low_s, high_ref)
     width = mine[0].shape[1]
     depth = parts_ref.shape[2]
     core = lax.rem(lax.axis_index("ctx"), 2)
@@ -294,7 +295,7 @@
         for which, ref in ((core, mine[j]), (1 - core, other[j])):
             at = (2 * lax.bitwise_xor(group, j) + which) * width
             at = pl.ds(pl.multiple_of(at, width), width)
-            for i, out_ref in enumerate(outs):
+            for i, into in enumerate(outs):
                 acc = sums[i][:, at].astype(jnp.float32)
                 for array in sums[2:] if i == 0 else ():
                     acc = acc + array[:, at].astype(jnp.float32)
@@ -305,7 +306,11 @@
                         ref[pl.ds(row, depth), :],
                         preferred_element_type=jnp.float32,
                     )
-                out_ref[:, at] = acc.astype(out_ref.dtype)
+                into[:, at] = acc.astype(into.dtype)
+    half = low_s.shape[0]
+    copy = pltpu.make_async_copy(low_s, out_ref.at[pl.ds(0, half), :], sem)
+    copy.start()
+    copy.wait()
 
 
 def near_sums(parts, mine, other, low, high, groups):
@@ -313,11 +318,12 @@
     return pl.pallas_call(
         functools.partial(near_kernel, groups),
         out_shape=[
-            jax.ShapeDtypeStruct((half, columns), jnp.bfloat16),
+            jax.ShapeDtypeStruct((2 * half, columns), jnp.bfloat16),
             jax.ShapeDtypeStruct((half, columns), jnp.float32),
         ],
+        scratch_shapes=[pltpu.VMEM((half, columns), jnp.bfloat16), pltpu.SemaphoreType.DMA],
         in_specs=[VMEM] * (2 * groups + 2 + len(low)),
-        out_specs=[VMEM] * 2,
+        out_specs=[HBM, VMEM],
         name="nsum",
         compiler_params=PARAMS,
         cost_estimate=pl.CostEstimate(
@@ -326,13 +332,12 @@
     )(parts, *mine, *other, low[0], high, *low[1:])
 
 
-def finish_kernel(low_ref, high_ref, *refs):
+def finish_kernel(rows_ref, high_ref, *refs):
     arrived, out_ref, made, sems = refs[:-3], refs[-3], refs[-2], refs[-1]
     half, columns = made.shape
-    count = sems.shape[0] - 1
+    count = sems.shape[0]
     tile = columns // count
-    copies = [pltpu.make_async_copy(low_ref, out_ref.at[pl.ds(0, half), :], sems.at[count])]
-    copies[0].start()
+    copies = []
     for i in range(count):
         at = pl.ds(i * tile, tile)
         acc = high_ref[:, at]
@@ -348,23 +353,24 @@
         copy.wait()
 
 
-def finish(low, high, arrived):
-    half, columns = low.shape
+def finish(rows, high, arrived):
+    half, columns = high.shape
     return pl.pallas_call(
         finish_kernel,
         out_shape=jax.ShapeDtypeStruct((2 * half, columns), jnp.bfloat16),
-        in_specs=[VMEM] * (2 + len(arrived)),
+        in_specs=[HBM] + [VMEM] * (1 + len(arrived)),
         out_specs=HBM,
         scratch_shapes=[
             pltpu.VMEM((half, columns), jnp.bfloat16),
-            pltpu.SemaphoreType.DMA((5,)),
+            pltpu.SemaphoreType.DMA((4,)),
         ],
+        input_output_aliases={0: 0},
         name="finish",
         compiler_params=PARAMS,
         cost_estimate=pl.CostEstimate(
             flops=3 * half * columns, bytes_accessed=10 * half * columns, transcendentals=0
         ),
-    )(low, high, *arrived)
+    )(rows, high, *arrived)
 
 
 def exchange_body(queries, attn_keys, attn_values, out_proj):

time: 158 us -> 158 us (level)
  no operation moved by 1% of the time
where the time goes in v3:
time: 158 us; the launch traced here: 157 us
  waiting for transfers between devices  92.4 us (58%)
  starting transfers between devices  36.8 us (23%)
  Pallas kernels  26.4 us (17%)
    ppermute x10, waiting for transfers between devices, line(): arrived = lax.ppermute(send, 'tp', pairs)  69.1 us
    ppermute x15, waiting for transfers between devices, swap(): got[j] = lax.ppermute(arrays[j], 'ctx', pairs)  23.2 us
    ppermute x15, starting transfers between devices, swap(): got[j] = lax.ppermute(arrays[j], 'ctx', pairs)  19 us
    ppermute x10, starting transfers between devices, line(): arrived = lax.ppermute(send, 'tp', pairs)  10.8 us
    pallas_call x4, Pallas kernels, hold(): pl.pallas_call(hold_kernel, out_shape=jax.ShapeDtypeStruct((rows, columns...  9.15 us
    pallas_call x8, Pallas kernels, project(): pl.pallas_call(functools.partial(project_kernel, groups), out_shape=jax.S...  5.91 us
    pallas_call x2, Pallas kernels, attention(): pl.pallas_call(functools.partial(attention_kernel, groups, phases), out_s...  4.78 us
    ppermute x1, starting transfers between devices, exchange_body(): share = lax.ppermute(share, 'tp', ends)  3.51 us
  transfers between devices with their start and end apart: 39, of which 14 were waited for; matrix products, arithmetic and copies ran while one was open for 1% of the time, Pallas kernels for 15%

profile of v3, /device:TPU:0, one launch (start us, length us, event | category | flops | bytes accessed | tf_op | source)
XLA Modules:
  0.0 157.1 jit_solution(17633154140913319763)
XLA Ops:
  0.0 1.3 shard_map.48
  1.3 3.0 %collective-permute-start.10 = (bf16[3,128,256]{2,1,0:T(8,128)(2,1)S(1)}, bf16[3,128,256]{2,1,0:T(8,128)(2,1)S(1)}, u32[]{:S(2)}, u32[]{:S(2)}) collective-permute-start(bf16[3,128,256]{2,1,0:T(8,128)(2,1)S(1)} %get-tuple-element.32), channel_id=1, source_target_pairs={{0,8},{4,12},{8,0},{12,4},{16,24},{20,28},{24,16},{28,20},{1,9},{5... | collective-permute-start | bytes 589832 | tf_op jit(solution)/shard_map/ppermute | solution.py:390
  4.3 1.5 collective-permute-start.11
  5.9 1.3 shard_map.46
  7.1 2.0 %collective-permute-start = (bf16[3,128,256]{2,1,0:T(8,128)(2,1)S(1)}, bf16[3,128,256]{2,1,0:T(8,128)(2,1)S(1)}, u32[]{:S(2)}, u32[]{:S(2)}) collective-permute-start(bf16[3,128,256]{2,1,0:T(8,128)(2,1)S(1)} %get-tuple-element.24), channel_id=1, source_target_pairs={{0,8},{4,12},{8,0},{12,4},{16,24},{20,28},{24,16},{28,20},{1,9},{5... | collective-permute-start | bytes 589832 | tf_op jit(solution)/shard_map/ppermute | solution.py:390
  9.1 0.9 collective-permute-done.10.refs_9_
  10.1 2.0 %collective-permute-start.1 = (bf16[3,128,256]{2,1,0:T(8,128)(2,1)S(1)}, bf16[3,128,256]{2,1,0:T(8,128)(2,1)S(1)}, u32[]{:S(2)}, u32[]{:S(2)}) collective-permute-start(bf16[3,128,256]{2,1,0:T(8,128)(2,1)S(1)} %get-tuple-element.25), channel_id=1, source_target_pairs={{0,16},{4,20},{8,24},{12,28},{16,0},{20,4},{24,8},{28,12},{1,17},{... | collective-permute-start | bytes 589832 | tf_op jit(solution)/shard_map/ppermute | solution.py:390
  12.1 3.2 %collective-permute-done.11.refs_10_ = bf16[3,128,256]{2,1,0:T(8,128)(2,1)S(1)} collective-permute-done((bf16[3,128,256]{2,1,0:T(8,128)(2,1)S(1)}, bf16[3,128,256]{2,1,0:T(8,128)(2,1)S(1)}, u32[]{:S(2)}, u32[]{:S(2)}) %collective-permute-start.11) | collective-permute-done | bytes 196640 | tf_op jit(solution)/shard_map/ppermute | solution.py:390
  15.3 0.6 collective-permute-start.2
  15.9 0.5 collective-permute-start.14
  16.4 2.1 %collective-permute-done.refs_1_ = bf16[3,128,256]{2,1,0:T(8,128)(2,1)S(1)} collective-permute-done((bf16[3,128,256]{2,1,0:T(8,128)(2,1)S(1)}, bf16[3,128,256]{2,1,0:T(8,128)(2,1)S(1)}, u32[]{:S(2)}, u32[]{:S(2)}) %collective-permute-start) | collective-permute-done | bytes 196640 | tf_op jit(solution)/shard_map/ppermute | solution.py:390
  18.5 4.8 %collective-permute-done.1.refs_2_ = bf16[3,128,256]{2,1,0:T(8,128)(2,1)S(1)} collective-permute-done((bf16[3,128,256]{2,1,0:T(8,128)(2,1)S(1)}, bf16[3,128,256]{2,1,0:T(8,128)(2,1)S(1)}, u32[]{:S(2)}, u32[]{:S(2)}) %collective-permute-start.1) | collective-permute-done | bytes 196640 | tf_op jit(solution)/shard_map/ppermute | solution.py:390
  23.3 0.5 collective-permute-start.4
  23.9 0.4 collective-permute-start.6
  24.3 1.0 piece.1
  25.4 2.3 %shard_map.53.refs_4_ = bf16[1024,2048]{1,0:T(8,128)(2,1)S(1)} custom-call(s32[1]{0:T(128)} %bitcast.9.place_ref, bf16[1024,8192]{1,0:T(8,128)(2,1)} %w_ref.9), custom_call_target="tpu_custom_call" | custom-call | bytes 8388608 | tf_op jit(solution)/shard_map/pallas_call | solution.py:234
  27.7 2.3 %shard_map.57.refs_4_ = bf16[1024,2048]{1,0:T(8,128)(2,1)S(1)} custom-call(s32[1]{0:T(128)} %bitcast.11.place_ref, bf16[1024,8192]{1,0:T(8,128)(2,1)} %w_ref.9), custom_call_target="tpu_custom_call" | custom-call | bytes 8388608 | tf_op jit(solution)/shard_map/pallas_call | solution.py:234
  30.0 2.3 %shard_map.55.refs_4_ = bf16[1024,2048]{1,0:T(8,128)(2,1)S(1)} custom-call(s32[1]{0:T(128)} %bitcast.10.place_ref, bf16[1024,8192]{1,0:T(8,128)(2,1)} %w_ref.9), custom_call_target="tpu_custom_call" | custom-call | bytes 8388608 | tf_op jit(solution)/shard_map/pallas_call | solution.py:234
  32.3 3.5 %collective-permute-start.21 = (bf16[1024,256]{1,0:T(8,128)(2,1)S(1)}, bf16[1024,256]{1,0:T(8,128)(2,1)S(1)}, u32[]{:S(2)}, u32[]{:S(2)}) collective-permute-start(bf16[1024,256]{1,0:T(8,128)(2,1)S(1)} %piece.1), channel_id=1, source_target_pairs={{0,1},{3,2},{4,5},{7,6},{8,9},{11,10},{12,13},{15,14},{16,17},{19,... | collective-permute-start | bytes 1572872 | tf_op jit(solution)/shard_map/ppermute | solution.py:413
  35.9 3.4 %shard_map.49 = (bf16[128,256]{1,0:T(8,128)(2,1)S(1)}, bf16[128,256]{1,0:T(8,128)(2,1)S(1)}, bf16[128,256]{1,0:T(8,128)(2,1)S(1)}, bf16[128,256]{1,0:T(8,128)(2,1)S(1)}) custom-call(bf16[3,128,256]{2,1,0:T(8,128)(2,1)S(1)} %get-tuple-element.23.refs_0_, bf16[3,128,256]{2,1,0:T(8,128)(2,1)S(1)} %collective-permute-done.refs_1_, ...), custom_call_target="tpu_custom_call" | custom-call | flops 872415232 | bytes 2097152 | tf_op jit(solution)/shard_map/pallas_call | solution.py:209
  39.3 0.9 collective-permute-start.17
  40.2 1.3 shard_map.47
  41.6 1.2 collective-permute-start.7
  42.8 1.5 collective-permute-start.8
  44.3 0.8 collective-permute-start.9
  45.1 0.8 collective-permute-done.7.refs_1_
  46.0 1.1 collective-permute-start.18
  47.1 0.9 collective-permute-done.8.refs_2_
  48.0 1.6 collective-permute-start.19
  49.5 0.5 collective-permute-done.9.refs_3_
  50.1 0.7 shard_map.58
  50.8 1.3 collective-permute-start.32
  52.3 0.9 collective-permute-done.19.refs_3_
  53.2 1.3 collective-permute-start.20
  54.5 0.7 shard_map.61
  55.2 1.3 collective-permute-start.37
  56.5 0.7 shard_map.56
  57.3 1.5 collective-permute-start.29
  58.8 0.7 shard_map.59
  59.6 0.8 shard_map.54
  60.3 0.7 shard_map.60
  61.1 1.3 collective-permute-start.34
  62.4 2.0 %collective-permute-done.32 = bf16[128,2048]{1,0:T(8,128)(2,1)S(1)} collective-permute-done((bf16[128,2048]{1,0:T(8,128)(2,1)S(1)}, bf16[128,2048]{1,0:T(8,128)(2,1)S(1)}, u32[]{:S(2)}, u32[]{:S(2)}) %collective-permute-start.32) | collective-permute-done | bytes 524320 | tf_op jit(solution)/shard_map/ppermute | solution.py:444
  64.6 33.6 %collective-permute-done.29 = bf16[128,2048]{1,0:T(8,128)(2,1)S(1)} collective-permute-done((bf16[128,2048]{1,0:T(8,128)(2,1)S(1)}, bf16[128,2048]{1,0:T(8,128)(2,1)S(1)}, u32[]{:S(2)}, u32[]{:S(2)}) %collective-permute-start.29) | collective-permute-done | bytes 524320 | tf_op jit(solution)/shard_map/ppermute | solution.py:444
  98.1 0.8 collective-permute-start.24
  99.1 6.9 %collective-permute-done.34 = bf16[128,2048]{1,0:T(8,128)(2,1)S(1)} collective-permute-done((bf16[128,2048]{1,0:T(8,128)(2,1)S(1)}, bf16[128,2048]{1,0:T(8,128)(2,1)S(1)}, u32[]{:S(2)}, u32[]{:S(2)}) %collective-permute-start.34) | collective-permute-done | bytes 524320 | tf_op jit(solution)/shard_map/ppermute | solution.py:444
  106.0 0.7 collective-permute-start.30
  106.8 0.8 collective-permute-start.23
  107.6 1.0 collective-permute-start.22
  108.7 0.7 collective-permute-start.35
  109.3 0.1 add_convert_fusion
  109.5 0.7 collective-permute-start.33
  110.4 9.0 %collective-permute-done.23.refs_3_ = bf16[1024,256]{1,0:T(8,128)(2,1)S(1)} collective-permute-done((bf16[1024,256]{1,0:T(8,128)(2,1)S(1)}, bf16[1024,256]{1,0:T(8,128)(2,1)S(1)}, u32[]{:S(2)}, u32[]{:S(2)}) %collective-permute-start.23) | collective-permute-done | bytes 524320 | tf_op jit(solution)/shard_map/ppermute | solution.py:390
  119.4 0.5 collective-permute-start.26
  120.0 1.3 collective-permute-start.31
  121.4 0.7 collective-permute-start.38
  122.1 1.3 collective-permute-start.36
  123.4 2.3 %shard_map.50.refs_4_ = bf16[1024,2048]{1,0:T(8,128)(2,1)S(1)} custom-call(s32[1]{0:T(128)} %bitcast.8.place_ref, bf16[1024,8192]{1,0:T(8,128)(2,1)} %w_ref.9), custom_call_target="tpu_custom_call" | custom-call | bytes 8388608 | tf_op jit(solution)/shard_map/pallas_call | solution.py:234
  125.7 0.7 shard_map.52.refs_10_
  126.4 0.7 shard_map.51.refs_9_
  127.2 17.8 %collective-permute-done.31.refs_11_ = bf16[128,2048]{1,0:T(8,128)(2,1)S(1)} collective-permute-done((bf16[128,2048]{1,0:T(8,128)(2,1)S(1)}, bf16[128,2048]{1,0:T(8,128)(2,1)S(1)}, u32[]{:S(2)}, u32[]{:S(2)}) %collective-permute-start.31) | collective-permute-done | bytes 524320 | tf_op jit(solution)/shard_map/ppermute | solution.py:444
  145.0 2.1 %nsum.1 = (bf16[256,2048]{1,0:T(8,128)(2,1)}, f32[128,2048]{1,0:T(8,128)S(1)}) custom-call(bf16[8,128,256]{2,1,0:T(8,128)(2,1)S(1)} %collective-permute-done.20.refs_0_, bf16[1024,256]{1,0:T(8,128)(2,1)S(1)} %collective-permute-done.21.refs_1_, bf16[1024,256]{1,0:T(8,128)(2,1)S(1)} %collective-permute-done.22.refs_2_, ...), custom_call_target="tpu_custom_call" | custom-call | flops 1073741824 | bytes 12582912 | tf_op jit(solution)/shard_map/nsum/pallas_call | solution.py:318
  147.1 8.9 %collective-permute-done.36.refs_0_ = bf16[128,2048]{1,0:T(8,128)(2,1)S(1)} collective-permute-done((bf16[128,2048]{1,0:T(8,128)(2,1)S(1)}, bf16[128,2048]{1,0:T(8,128)(2,1)S(1)}, u32[]{:S(2)}, u32[]{:S(2)}) %collective-permute-start.36) | collective-permute-done | bytes 524320 | tf_op jit(solution)/shard_map/ppermute | solution.py:444
  156.0 0.9 finish.1
  (47 shorter events, 0.9 us)
Async XLA Ops:
  1.3 8.8 %collective-permute-start.10 = (bf16[3,128,256]{2,1,0:T(8,128)(2,1)S(1)}, bf16[3,128,256]{2,1,0:T(8,128)(2,1)S(1)}, u32[]{:S(2)}, u32[]{:S(2)}) collective-permute-start(bf16[3,128,256]{2,1,0:T(8,128)(2,1)S(1)} %get-tuple-element.32), channel_id=1, source_target_pairs={{0,8},{4,12},{8,0},{12,4},{16,24},{20,28},{24,16},{28,20},{1,9},{5... | collective-permute-start | bytes 589832 | tf_op jit(solution)/shard_map/ppermute | solution.py:390
  4.3 11.0 %collective-permute-start.11 = (bf16[3,128,256]{2,1,0:T(8,128)(2,1)S(1)}, bf16[3,128,256]{2,1,0:T(8,128)(2,1)S(1)}, u32[]{:S(2)}, u32[]{:S(2)}) collective-permute-start(bf16[3,128,256]{2,1,0:T(8,128)(2,1)S(1)} %get-tuple-element.33), channel_id=1, source_target_pairs={{0,16},{4,20},{8,24},{12,28},{16,0},{20,4},{24,8},{28,12},{1,17},{... | collective-permute-start | bytes 589832 | tf_op jit(solution)/shard_map/ppermute | solution.py:390
  5.8 10.1 %collective-permute-start.12 = (bf16[3,128,256]{2,1,0:T(8,128)(2,1)S(1)}, bf16[3,128,256]{2,1,0:T(8,128)(2,1)S(1)}, u32[]{:S(2)}, u32[]{:S(2)}) collective-permute-start(bf16[3,128,256]{2,1,0:T(8,128)(2,1)S(1)} %get-tuple-element.34), channel_id=1, source_target_pairs={{0,24},{4,28},{8,16},{12,20},{16,8},{20,12},{24,0},{28,4},{1,25},{... | collective-permute-start | bytes 589832 | tf_op jit(solution)/shard_map/ppermute | solution.py:390
  5.8 10.1 %collective-permute-start.13 = (bf16[3,128,256]{2,1,0:T(8,128)(2,1)S(1)}, bf16[3,128,256]{2,1,0:T(8,128)(2,1)S(1)}, u32[]{:S(2)}, u32[]{:S(2)}) collective-permute-start(bf16[3,128,256]{2,1,0:T(8,128)(2,1)S(1)} %get-tuple-element.31.refs_8_), channel_id=1, source_target_pairs={{0,4},{4,0},{8,12},{12,8},{16,20},{20,16},{24,28},{28,24},{1,5},{5... | collective-permute-start | bytes 589832 | tf_op jit(solution)/shard_map/ppermute | solution.py:394
  7.1 11.4 %collective-permute-start = (bf16[3,128,256]{2,1,0:T(8,128)(2,1)S(1)}, bf16[3,128,256]{2,1,0:T(8,128)(2,1)S(1)}, u32[]{:S(2)}, u32[]{:S(2)}) collective-permute-start(bf16[3,128,256]{2,1,0:T(8,128)(2,1)S(1)} %get-tuple-element.24), channel_id=1, source_target_pairs={{0,8},{4,12},{8,0},{12,4},{16,24},{20,28},{24,16},{28,20},{1,9},{5... | collective-permute-start | bytes 589832 | tf_op jit(solution)/shard_map/ppermute | solution.py:390
  10.1 13.2 %collective-permute-start.1 = (bf16[3,128,256]{2,1,0:T(8,128)(2,1)S(1)}, bf16[3,128,256]{2,1,0:T(8,128)(2,1)S(1)}, u32[]{:S(2)}, u32[]{:S(2)}) collective-permute-start(bf16[3,128,256]{2,1,0:T(8,128)(2,1)S(1)} %get-tuple-element.25), channel_id=1, source_target_pairs={{0,16},{4,20},{8,24},{12,28},{16,0},{20,4},{24,8},{28,12},{1,17},{... | collective-permute-start | bytes 589832 | tf_op jit(solution)/shard_map/ppermute | solution.py:390
  15.3 8.0 %collective-permute-start.2 = (bf16[3,128,256]{2,1,0:T(8,128)(2,1)S(1)}, bf16[3,128,256]{2,1,0:T(8,128)(2,1)S(1)}, u32[]{:S(2)}, u32[]{:S(2)}) collective-permute-start(bf16[3,128,256]{2,1,0:T(8,128)(2,1)S(1)} %get-tuple-element.26), channel_id=1, source_target_pairs={{0,24},{4,28},{8,16},{12,20},{16,8},{20,12},{24,0},{28,4},{1,25},{... | collective-permute-start | bytes 589832 | tf_op jit(solution)/shard_map/ppermute | solution.py:390
  15.9 7.9 %collective-permute-start.3 = (bf16[3,128,256]{2,1,0:T(8,128)(2,1)S(1)}, bf16[3,128,256]{2,1,0:T(8,128)(2,1)S(1)}, u32[]{:S(2)}, u32[]{:S(2)}) collective-permute-start(bf16[3,128,256]{2,1,0:T(8,128)(2,1)S(1)} %get-tuple-element.23.refs_0_), channel_id=1, source_target_pairs={{0,4},{4,0},{8,12},{12,8},{16,20},{20,16},{24,28},{28,24},{1,5},{5... | collective-permute-start | bytes 589832 | tf_op jit(solution)/shard_map/ppermute | solution.py:394
  15.9 8.0 %collective-permute-start.14 = (bf16[3,128,256]{2,1,0:T(8,128)(2,1)S(1)}, bf16[3,128,256]{2,1,0:T(8,128)(2,1)S(1)}, u32[]{:S(2)}, u32[]{:S(2)}) collective-permute-start(bf16[3,128,256]{2,1,0:T(8,128)(2,1)S(1)} %collective-permute-done.10.refs_9_), channel_id=1, source_target_pairs={{0,4},{4,0},{8,12},{12,8},{16,20},{20,16},{24,28},{28,24},{1,5},{5... | collective-permute-start | bytes 589832 | tf_op jit(solution)/shard_map/ppermute | solution.py:394
  18.5 13.8 %collective-permute-start.15 = (bf16[3,128,256]{2,1,0:T(8,128)(2,1)S(1)}, bf16[3,128,256]{2,1,0:T(8,128)(2,1)S(1)}, u32[]{:S(2)}, u32[]{:S(2)}) collective-permute-start(bf16[3,128,256]{2,1,0:T(8,128)(2,1)S(1)} %collective-permute-done.11.refs_10_), channel_id=1, source_target_pairs={{0,4},{4,0},{8,12},{12,8},{16,20},{20,16},{24,28},{28,24},{1,5},{5... | collective-permute-start | bytes 589832 | tf_op jit(solution)/shard_map/ppermute | solution.py:394
  23.3 12.5 %collective-permute-start.16 = (bf16[3,128,256]{2,1,0:T(8,128)(2,1)S(1)}, bf16[3,128,256]{2,1,0:T(8,128)(2,1)S(1)}, u32[]{:S(2)}, u32[]{:S(2)}) collective-permute-start(bf16[3,128,256]{2,1,0:T(8,128)(2,1)S(1)} %collective-permute-done.12.refs_11_), channel_id=1, source_target_pairs={{0,4},{4,0},{8,12},{12,8},{16,20},{20,16},{24,28},{28,24},{1,5},{5... | collective-permute-start | bytes 589832 | tf_op jit(solution)/shard_map/ppermute | solution.py:394
  23.3 12.5 %collective-permute-start.4 = (bf16[3,128,256]{2,1,0:T(8,128)(2,1)S(1)}, bf16[3,128,256]{2,1,0:T(8,128)(2,1)S(1)}, u32[]{:S(2)}, u32[]{:S(2)}) collective-permute-start(bf16[3,128,256]{2,1,0:T(8,128)(2,1)S(1)} %collective-permute-done.refs_1_), channel_id=1, source_target_pairs={{0,4},{4,0},{8,12},{12,8},{16,20},{20,16},{24,28},{28,24},{1,5},{5... | collective-permute-start | bytes 589832 | tf_op jit(solution)/shard_map/ppermute | solution.py:394
  23.8 12.0 %collective-permute-start.5 = (bf16[3,128,256]{2,1,0:T(8,128)(2,1)S(1)}, bf16[3,128,256]{2,1,0:T(8,128)(2,1)S(1)}, u32[]{:S(2)}, u32[]{:S(2)}) collective-permute-start(bf16[3,128,256]{2,1,0:T(8,128)(2,1)S(1)} %collective-permute-done.1.refs_2_), channel_id=1, source_target_pairs={{0,4},{4,0},{8,12},{12,8},{16,20},{20,16},{24,28},{28,24},{1,5},{5... | collective-permute-start | bytes 589832 | tf_op jit(solution)/shard_map/ppermute | solution.py:394
  23.9 12.0 %collective-permute-start.6 = (bf16[3,128,256]{2,1,0:T(8,128)(2,1)S(1)}, bf16[3,128,256]{2,1,0:T(8,128)(2,1)S(1)}, u32[]{:S(2)}, u32[]{:S(2)}) collective-permute-start(bf16[3,128,256]{2,1,0:T(8,128)(2,1)S(1)} %collective-permute-done.2.refs_3_), channel_id=1, source_target_pairs={{0,4},{4,0},{8,12},{12,8},{16,20},{20,16},{24,28},{28,24},{1,5},{5... | collective-permute-start | bytes 589832 | tf_op jit(solution)/shard_map/ppermute | solution.py:394
  32.3 28.8 %collective-permute-start.21 = (bf16[1024,256]{1,0:T(8,128)(2,1)S(1)}, bf16[1024,256]{1,0:T(8,128)(2,1)S(1)}, u32[]{:S(2)}, u32[]{:S(2)}) collective-permute-start(bf16[1024,256]{1,0:T(8,128)(2,1)S(1)} %piece.1), channel_id=1, source_target_pairs={{0,1},{3,2},{4,5},{7,6},{8,9},{11,10},{12,13},{15,14},{16,17},{19,... | collective-permute-start | bytes 1572872 | tf_op jit(solution)/shard_map/ppermute | solution.py:413
  39.3 12.9 %collective-permute-start.17 = (bf16[128,256]{1,0:T(8,128)(2,1)S(1)}, bf16[128,256]{1,0:T(8,128)(2,1)S(1)}, u32[]{:S(2)}, u32[]{:S(2)}) collective-permute-start(bf16[128,256]{1,0:T(8,128)(2,1)S(1)} %get-tuple-element.36), channel_id=1, source_target_pairs={{0,8},{4,12},{8,0},{12,4},{16,24},{20,28},{24,16},{28,20},{1,9},{5... | collective-permute-start | bytes 196616 | tf_op jit(solution)/shard_map/ppermute | solution.py:390
  41.6 4.4 %collective-permute-start.7 = (bf16[128,256]{1,0:T(8,128)(2,1)S(1)}, bf16[128,256]{1,0:T(8,128)(2,1)S(1)}, u32[]{:S(2)}, u32[]{:S(2)}) collective-permute-start(bf16[128,256]{1,0:T(8,128)(2,1)S(1)} %get-tuple-element.28), channel_id=1, source_target_pairs={{0,8},{4,12},{8,0},{12,4},{16,24},{20,28},{24,16},{28,20},{1,9},{5... | collective-permute-start | bytes 196616 | tf_op jit(solution)/shard_map/ppermute | solution.py:390
  42.8 5.2 %collective-permute-start.8 = (bf16[128,256]{1,0:T(8,128)(2,1)S(1)}, bf16[128,256]{1,0:T(8,128)(2,1)S(1)}, u32[]{:S(2)}, u32[]{:S(2)}) collective-permute-start(bf16[128,256]{1,0:T(8,128)(2,1)S(1)} %get-tuple-element.29), channel_id=1, source_target_pairs={{0,16},{4,20},{8,24},{12,28},{16,0},{20,4},{24,8},{28,12},{1,17},{... | collective-permute-start | bytes 196616 | tf_op jit(solution)/shard_map/ppermute | solution.py:390
  44.3 5.8 %collective-permute-start.9 = (bf16[128,256]{1,0:T(8,128)(2,1)S(1)}, bf16[128,256]{1,0:T(8,128)(2,1)S(1)}, u32[]{:S(2)}, u32[]{:S(2)}) collective-permute-start(bf16[128,256]{1,0:T(8,128)(2,1)S(1)} %get-tuple-element.30), channel_id=1, source_target_pairs={{0,24},{4,28},{8,16},{12,20},{16,8},{20,12},{24,0},{28,4},{1,25},{... | collective-permute-start | bytes 196616 | tf_op jit(solution)/shard_map/ppermute | solution.py:390
  46.0 6.3 %collective-permute-start.18 = (bf16[128,256]{1,0:T(8,128)(2,1)S(1)}, bf16[128,256]{1,0:T(8,128)(2,1)S(1)}, u32[]{:S(2)}, u32[]{:S(2)}) collective-permute-start(bf16[128,256]{1,0:T(8,128)(2,1)S(1)} %get-tuple-element.37), channel_id=1, source_target_pairs={{0,16},{4,20},{8,24},{12,28},{16,0},{20,4},{24,8},{28,12},{1,17},{... | collective-permute-start | bytes 196616 | tf_op jit(solution)/shard_map/ppermute | solution.py:390
  48.0 5.2 %collective-permute-start.19 = (bf16[128,256]{1,0:T(8,128)(2,1)S(1)}, bf16[128,256]{1,0:T(8,128)(2,1)S(1)}, u32[]{:S(2)}, u32[]{:S(2)}) collective-permute-start(bf16[128,256]{1,0:T(8,128)(2,1)S(1)} %get-tuple-element.38), channel_id=1, source_target_pairs={{0,24},{4,28},{8,16},{12,20},{16,8},{20,12},{24,0},{28,4},{1,25},{... | collective-permute-start | bytes 196616 | tf_op jit(solution)/shard_map/ppermute | solution.py:390
  50.8 13.6 %collective-permute-start.32 = (bf16[128,2048]{1,0:T(8,128)(2,1)S(1)}, bf16[128,2048]{1,0:T(8,128)(2,1)S(1)}, u32[]{:S(2)}, u32[]{:S(2)}) collective-permute-start(bf16[128,2048]{1,0:T(8,128)(2,1)S(1)} %shard_map.58), channel_id=1, source_target_pairs={{0,1},{3,2},{4,5},{7,6},{8,9},{11,10},{12,13},{15,14},{16,17},{19,... | collective-permute-start | bytes 1572872 | tf_op jit(solution)/shard_map/ppermute | solution.py:444
  53.2 53.7 %collective-permute-start.20 = (bf16[8,128,256]{2,1,0:T(8,128)(2,1)S(1)}, bf16[8,128,256]{2,1,0:T(8,128)(2,1)S(1)}, u32[]{:S(2)}, u32[]{:S(2)}) collective-permute-start(bf16[8,128,256]{2,1,0:T(8,128)(2,1)S(1)} %bitcast_dynamic-update-slice_fusion), channel_id=1, source_target_pairs={{0,1},{3,2},{4,5},{7,6},{8,9},{11,10},{12,13},{15,14},{16,17},{19,... | collective-permute-start | bytes 1572872 | tf_op jit(solution)/shard_map/ppermute | solution.py:450
  55.2 52.4 %collective-permute-start.37 = (bf16[128,2048]{1,0:T(8,128)(2,1)S(1)}, bf16[128,2048]{1,0:T(8,128)(2,1)S(1)}, u32[]{:S(2)}, u32[]{:S(2)}) collective-permute-start(bf16[128,2048]{1,0:T(8,128)(2,1)S(1)} %shard_map.61), channel_id=1, source_target_pairs={{0,1},{3,2},{4,5},{7,6},{8,9},{11,10},{12,13},{15,14},{16,17},{19,... | collective-permute-start | bytes 1572872 | tf_op jit(solution)/shard_map/ppermute | solution.py:444
  57.3 40.8 %collective-permute-start.29 = (bf16[128,2048]{1,0:T(8,128)(2,1)S(1)}, bf16[128,2048]{1,0:T(8,128)(2,1)S(1)}, u32[]{:S(2)}, u32[]{:S(2)}) collective-permute-start(bf16[128,2048]{1,0:T(8,128)(2,1)S(1)} %shard_map.56), channel_id=1, source_target_pairs={{0,1},{3,2},{4,5},{7,6},{8,9},{11,10},{12,13},{15,14},{16,17},{19,... | collective-permute-start | bytes 1572872 | tf_op jit(solution)/shard_map/ppermute | solution.py:444
  61.1 44.9 %collective-permute-start.34 = (bf16[128,2048]{1,0:T(8,128)(2,1)S(1)}, bf16[128,2048]{1,0:T(8,128)(2,1)S(1)}, u32[]{:S(2)}, u32[]{:S(2)}) collective-permute-start(bf16[128,2048]{1,0:T(8,128)(2,1)S(1)} %shard_map.60), channel_id=1, source_target_pairs={{0,1},{3,2},{4,5},{7,6},{8,9},{11,10},{12,13},{15,14},{16,17},{19,... | collective-permute-start | bytes 1572872 | tf_op jit(solution)/shard_map/ppermute | solution.py:444
  64.4 44.2 %collective-permute-start.25 = (bf16[1024,256]{1,0:T(8,128)(2,1)S(1)}, bf16[1024,256]{1,0:T(8,128)(2,1)S(1)}, u32[]{:S(2)}, u32[]{:S(2)}) collective-permute-start(bf16[1024,256]{1,0:T(8,128)(2,1)S(1)} %collective-permute-done.21.refs_1_), channel_id=1, source_target_pairs={{0,4},{4,0},{8,12},{12,8},{16,20},{20,16},{24,28},{28,24},{1,5},{5... | collective-permute-start | bytes 1572872 | tf_op jit(solution)/shard_map/ppermute | solution.py:394
  98.1 11.4 %collective-permute-start.24 = (bf16[1024,256]{1,0:T(8,128)(2,1)S(1)}, bf16[1024,256]{1,0:T(8,128)(2,1)S(1)}, u32[]{:S(2)}, u32[]{:S(2)}) collective-permute-start(bf16[1024,256]{1,0:T(8,128)(2,1)S(1)} %collective-permute-done.21.refs_1_), channel_id=1, source_target_pairs={{0,24},{4,28},{8,16},{12,20},{16,8},{20,12},{24,0},{28,4},{1,25},{... | collective-permute-start | bytes 1572872 | tf_op jit(solution)/shard_map/ppermute | solution.py:390
  106.0 4.2 %collective-permute-start.30 = (bf16[128,2048]{1,0:T(8,128)(2,1)S(1)}, bf16[128,2048]{1,0:T(8,128)(2,1)S(1)}, u32[]{:S(2)}, u32[]{:S(2)}) collective-permute-start(bf16[128,2048]{1,0:T(8,128)(2,1)S(1)} %add_convert_fusion.5), channel_id=1, source_target_pairs={{1,2},{2,1},{5,6},{6,5},{9,10},{10,9},{13,14},{14,13},{17,18},{18,... | collective-permute-start | bytes 1572872 | tf_op jit(solution)/shard_map/ppermute | solution.py:444
  106.8 12.6 %collective-permute-start.23 = (bf16[1024,256]{1,0:T(8,128)(2,1)S(1)}, bf16[1024,256]{1,0:T(8,128)(2,1)S(1)}, u32[]{:S(2)}, u32[]{:S(2)}) collective-permute-start(bf16[1024,256]{1,0:T(8,128)(2,1)S(1)} %collective-permute-done.21.refs_1_), channel_id=1, source_target_pairs={{0,16},{4,20},{8,24},{12,28},{16,0},{20,4},{24,8},{28,12},{1,17},{... | collective-permute-start | bytes 1572872 | tf_op jit(solution)/shard_map/ppermute | solution.py:390
  107.6 11.8 %collective-permute-start.22 = (bf16[1024,256]{1,0:T(8,128)(2,1)S(1)}, bf16[1024,256]{1,0:T(8,128)(2,1)S(1)}, u32[]{:S(2)}, u32[]{:S(2)}) collective-permute-start(bf16[1024,256]{1,0:T(8,128)(2,1)S(1)} %collective-permute-done.21.refs_1_), channel_id=1, source_target_pairs={{0,8},{4,12},{8,0},{12,4},{16,24},{20,28},{24,16},{28,20},{1,9},{5... | collective-permute-start | bytes 1572872 | tf_op jit(solution)/shard_map/ppermute | solution.py:390
  108.7 11.3 %collective-permute-start.35 = (bf16[128,2048]{1,0:T(8,128)(2,1)S(1)}, bf16[128,2048]{1,0:T(8,128)(2,1)S(1)}, u32[]{:S(2)}, u32[]{:S(2)}) collective-permute-start(bf16[128,2048]{1,0:T(8,128)(2,1)S(1)} %add_convert_fusion.2), channel_id=1, source_target_pairs={{1,2},{2,1},{5,6},{6,5},{9,10},{10,9},{13,14},{14,13},{17,18},{18,... | collective-permute-start | bytes 1572872 | tf_op jit(solution)/shard_map/ppermute | solution.py:444
  109.5 11.9 %collective-permute-start.33 = (bf16[128,2048]{1,0:T(8,128)(2,1)S(1)}, bf16[128,2048]{1,0:T(8,128)(2,1)S(1)}, u32[]{:S(2)}, u32[]{:S(2)}) collective-permute-start(bf16[128,2048]{1,0:T(8,128)(2,1)S(1)} %add_convert_fusion.3), channel_id=1, source_target_pairs={{1,2},{2,1},{5,6},{6,5},{9,10},{10,9},{13,14},{14,13},{17,18},{18,... | collective-permute-start | bytes 1572872 | tf_op jit(solution)/shard_map/ppermute | solution.py:444
  110.2 11.9 %collective-permute-start.28 = (bf16[1024,256]{1,0:T(8,128)(2,1)S(1)}, bf16[1024,256]{1,0:T(8,128)(2,1)S(1)}, u32[]{:S(2)}, u32[]{:S(2)}) collective-permute-start(bf16[1024,256]{1,0:T(8,128)(2,1)S(1)} %collective-permute-done.24.refs_4_), channel_id=1, source_target_pairs={{0,4},{4,0},{8,12},{12,8},{16,20},{20,16},{24,28},{28,24},{1,5},{5... | collective-permute-start | bytes 1572872 | tf_op jit(solution)/shard_map/ppermute | solution.py:394
  119.4 7.8 %collective-permute-start.27 = (bf16[1024,256]{1,0:T(8,128)(2,1)S(1)}, bf16[1024,256]{1,0:T(8,128)(2,1)S(1)}, u32[]{:S(2)}, u32[]{:S(2)}) collective-permute-start(bf16[1024,256]{1,0:T(8,128)(2,1)S(1)} %collective-permute-done.23.refs_3_), channel_id=1, source_target_pairs={{0,4},{4,0},{8,12},{12,8},{16,20},{20,16},{24,28},{28,24},{1,5},{5... | collective-permute-start | bytes 1572872 | tf_op jit(solution)/shard_map/ppermute | solution.py:394
  119.4 7.8 %collective-permute-start.26 = (bf16[1024,256]{1,0:T(8,128)(2,1)S(1)}, bf16[1024,256]{1,0:T(8,128)(2,1)S(1)}, u32[]{:S(2)}, u32[]{:S(2)}) collective-permute-start(bf16[1024,256]{1,0:T(8,128)(2,1)S(1)} %collective-permute-done.22.refs_2_), channel_id=1, source_target_pairs={{0,4},{4,0},{8,12},{12,8},{16,20},{20,16},{24,28},{28,24},{1,5},{5... | collective-permute-start | bytes 1572872 | tf_op jit(solution)/shard_map/ppermute | solution.py:394
  120.0 25.0 %collective-permute-start.31 = (bf16[128,2048]{1,0:T(8,128)(2,1)S(1)}, bf16[128,2048]{1,0:T(8,128)(2,1)S(1)}, u32[]{:S(2)}, u32[]{:S(2)}) collective-permute-start(bf16[128,2048]{1,0:T(8,128)(2,1)S(1)} %add_convert_fusion.4), channel_id=1, source_target_pairs={{2,3},{1,0},{6,7},{5,4},{10,11},{9,8},{14,15},{13,12},{18,19},{17,... | collective-permute-start | bytes 1572872 | tf_op jit(solution)/shard_map/ppermute | solution.py:444
  121.4 25.7 %collective-permute-start.38 = (bf16[128,2048]{1,0:T(8,128)(2,1)S(1)}, bf16[128,2048]{1,0:T(8,128)(2,1)S(1)}, u32[]{:S(2)}, u32[]{:S(2)}) collective-permute-start(bf16[128,2048]{1,0:T(8,128)(2,1)S(1)} %add_convert_fusion), channel_id=1, source_target_pairs={{1,2},{2,1},{5,6},{6,5},{9,10},{10,9},{13,14},{14,13},{17,18},{18,... | collective-permute-start | bytes 1572872 | tf_op jit(solution)/shard_map/ppermute | solution.py:444
  122.1 33.9 %collective-permute-start.36 = (bf16[128,2048]{1,0:T(8,128)(2,1)S(1)}, bf16[128,2048]{1,0:T(8,128)(2,1)S(1)}, u32[]{:S(2)}, u32[]{:S(2)}) collective-permute-start(bf16[128,2048]{1,0:T(8,128)(2,1)S(1)} %add_convert_fusion.1), channel_id=1, source_target_pairs={{2,3},{1,0},{6,7},{5,4},{10,11},{9,8},{14,15},{13,12},{18,19},{17,... | collective-permute-start | bytes 1572872 | tf_op jit(solution)/shard_map/ppermute | solution.py:444
